TPU v7x, 32 devices: a whole 2x2x4 slice. The times are simulated.
32 devices in a mesh: head: 8 (over z, y), fsdp: 4 (over x, core).
Axes of the slice: x: 2, y: 2, z: 4, core: 2. Of those that a mesh axis runs over, the one named last changes fastest.
Arguments:
- hidden: bfloat16 [4, 1024, 2048], P('fsdp', 'head'), may hold values from -6 to 6
- w_qkv: bfloat16 [2048, 6144], P(('head', 'fsdp')), may hold values from -0.125 to 0.125
- w_out: bfloat16 [2048, 2048], P(('head', 'fsdp')), may hold values from -0.75 to 0.75
- w_router: bfloat16 [2048, 16], P(('head', 'fsdp')), may hold values from -0.0625 to 0.0625
- g_attn: bfloat16 [2048], P(('head', 'fsdp')), may hold values from 0.099609375 to 1.8984375
- g_ffn: bfloat16 [2048], P(('head', 'fsdp')), may hold values from 0.099609375 to 1.8984375
- g_q: bfloat16 [2048], P(('head', 'fsdp')), may hold values from 0.69921875 to 2
- g_k: bfloat16 [2048], P(('head', 'fsdp')), may hold values from 0.69921875 to 2
- w_gate: bfloat16 [16, 2048, 1024], P('head', 'fsdp'), may hold values from -0.125 to 0.125
- w_up: bfloat16 [16, 2048, 1024], P('head', 'fsdp'), may hold values from -0.125 to 0.125
- w_down: bfloat16 [16, 1024, 2048], P('head', 'fsdp'), may hold values from -0.75 to 0.75
- lengths: int32 [4], P('fsdp'), may hold values from 256 to 1024, as said below
- routes: int32 [4, 1024, 8], P('fsdp', 'head'), may hold values from 0 to 15, all different within a row; in each aligned block of 128 rows (0 to 127, 128 to 255, ..., all dimensions but the last counted through in order) at most 96 rows name the same one
- route_codes: int32 [4, 1024, 8], P('fsdp', 'head'), may hold values from -384 to 383
- cotangent: bfloat16 [4, 1024, 2048], P('fsdp', 'head'), may hold values from -6 to 6
Outputs:
- out: bfloat16 [4, 1024, 2048], P('fsdp', 'head')
- d_hidden: float32 [4, 1024, 2048], P('fsdp', 'head')
- d_w_qkv: float32 [2048, 6144], P(('head', 'fsdp'))
- d_w_out: float32 [2048, 2048], P(('head', 'fsdp'))
- d_w_router: float32 [2048, 16], P(('head', 'fsdp'))
- d_g_attn: float32 [2048], P(('head', 'fsdp'))
- d_g_ffn: float32 [2048], P(('head', 'fsdp'))
- d_g_q: float32 [2048], P(('head', 'fsdp'))
- d_g_k: float32 [2048], P(('head', 'fsdp'))
- d_w_gate: float32 [16, 2048, 1024], P('head', 'fsdp')
- d_w_up: float32 [16, 2048, 1024], P('head', 'fsdp')
- d_w_down: float32 [16, 1024, 2048], P('head', 'fsdp')
Inputs may be any that keep to these rules, and one draw needn't show every extreme that they name: `lengths`: keys at positions at or after a sequence's length are masked. Some sequence has 1024 valid slots, some 1024 // 4. Each token names 8 different experts. In the 128 tokens of one device no expert is named by more than 96 routes, and some expert reaches 96.
All inputs are finite; a program needn't handle non-finite values.
Results may differ from a plain program's by a relative error of at most 0.018.
Values may be sent and summed in bfloat16 or wider, within the bound.
A program may use at most 256 MiB of HBM per device.

v0:
```python
import math
import jax
import jax.numpy as jnp
from jax import lax
from jax.sharding import PartitionSpec as P

HEADS = 16
HD = 128
FF = 1024
TOP = 8
EXP_DEV = 2
EPS = 1e-06
ROPE_BASE = 10000.0
NEGATIVE = -1e30
BF = jnp.bfloat16
F32 = jnp.float32


def ring_head(n, k):
    k %= n
    return 2 * k if k < n // 2 else 2 * n - 1 - 2 * k


def ring_links(n):
    right = [(ring_head(n, k), ring_head(n, k + 1)) for k in range(n)]
    return (right, [(b, a) for a, b in right])


def ring_place():
    n = lax.axis_size("head")
    me = lax.axis_index("head")
    odd = me % 2
    return (1 - odd) * (me // 2) + odd * (n - 1 - me // 2)


def head_at(offset):
    n = lax.axis_size("head")
    k = (ring_place() + offset + n) % n
    down = k // (n // 2)
    return (1 - down) * 2 * k + down * (2 * n - 1 - 2 * k)


def gather_ring(block):
    n = lax.axis_size("head")
    right, left = ring_links(n)
    half = n // 2
    rows = block.shape[0] // 2
    out = jnp.zeros((n,) + block.shape, block.dtype)

    def put(out, piece, offset):
        return lax.dynamic_update_slice_in_dim(out, piece[None], head_at(offset), 0)

    out = put(out, block, 0)
    r = l = block
    for step in range(1, half):
        r = lax.ppermute(r, "head", right)
        l = lax.ppermute(l, "head", left)
        out = put(out, r, -step)
        out = put(out, l, step)
    a = lax.ppermute(r[:rows], "head", right)
    b = lax.ppermute(l[rows:], "head", left)
    return put(out, jnp.concatenate([a, b], 0), half)


def scatter_ring(parts):
    n = lax.axis_size("head")
    right, left = ring_links(n)
    half = n // 2
    rows = parts.shape[1] // 2

    def piece(offset):
        return lax.dynamic_index_in_dim(parts, head_at(offset), 0, keepdims=False)

    far = piece(half)
    r = lax.ppermute(far[:rows], "head", right)
    l = lax.ppermute(far[rows:], "head", left)
    for step in range(half - 1, 0, -1):
        br = piece(step).astype(F32)
        bl = piece(-step).astype(F32)
        if step == half - 1:
            br = jnp.concatenate([br[:rows] + r.astype(F32), br[rows:]], 0)
            bl = jnp.concatenate([bl[:rows], bl[rows:] + l.astype(F32)], 0)
        else:
            br = br + r.astype(F32)
            bl = bl + l.astype(F32)
        r = lax.ppermute(br.astype(BF), "head", right)
        l = lax.ppermute(bl.astype(BF), "head", left)
    return piece(0).astype(F32) + r.astype(F32) + l.astype(F32)


def rotate(values, cosine, sine):
    half = HD // 2
    shaped = values.reshape(values.shape[0], -1, HD)
    first = shaped[..., :half]
    second = shaped[..., half:]
    turned = jnp.concatenate(
        [first * cosine - second * sine, second * cosine + first * sine], axis=-1
    )
    return turned.reshape(values.shape)


def dot(a, b, dims=((1,), (0,))):
    return lax.dot_general(a, b, (dims, ((), ())), preferred_element_type=F32)


NT = ((1,), (1,))
TN = ((0,), (0,))


def body(
    hidden,
    w_qkv,
    w_out,
    w_router,
    g_attn,
    g_ffn,
    g_q,
    g_k,
    w_gate,
    w_up,
    w_down,
    lengths,
    routes,
    route_codes,
    cotangent,
):
    n = lax.axis_size("head")
    m = lax.axis_size("fsdp")
    me = lax.axis_index("head")
    rows = hidden.shape[1]
    width = hidden.shape[2]
    seq = rows * n
    lh = HEADS // n
    dh = lh * HD
    experts = EXP_DEV * n
    shard = w_qkv.shape[0]
    scale = 1.0 / math.sqrt(HD)
    both = ("head", "fsdp")
    small = jnp.concatenate(
        [w_router, g_attn[:, None], g_ffn[:, None], g_q[:, None], g_k[:, None]], axis=1
    )
    small = lax.all_gather(small, both, axis=0, tiled=True)
    router = small[:, :experts]
    gain_attn = small[:, experts].astype(F32)
    gain_ffn = small[:, experts + 1].astype(F32)
    gains_q = lax.dynamic_slice_in_dim(small[:, experts + 2], me * dh, dh, 0).astype(F32)
    gains_k = lax.dynamic_slice_in_dim(small[:, experts + 3], me * dh, dh, 0).astype(F32)
    cols = w_qkv.reshape(shard, 3, n, dh).transpose(2, 0, 1, 3).reshape(n, shard, 3 * dh)
    cols = lax.all_to_all(cols, "head", split_axis=0, concat_axis=0, tiled=True)
    qkv = lax.all_gather(cols, "fsdp", axis=1, tiled=True).reshape(width, 3 * dh)
    tokens_all = gather_ring(hidden[0]).reshape(seq, width)
    info = gather_ring(jnp.concatenate([routes[0], route_codes[0]], axis=1)).reshape(seq, 2 * TOP)
    full_out = lax.all_gather(w_out, both, axis=0, tiled=True)
    full_gate = lax.all_gather(w_gate, "fsdp", axis=1, tiled=True)
    full_up = lax.all_gather(w_up, "fsdp", axis=1, tiled=True)
    full_down = lax.all_gather(w_down, "fsdp", axis=1, tiled=True)

    def own(values):
        return lax.dynamic_slice_in_dim(values, me * rows, rows, 0)

    def inverse_rms(values):
        return lax.rsqrt(jnp.mean(values * values, axis=-1, keepdims=True) + EPS)

    wide = tokens_all.astype(F32)
    attn_input = (wide * inverse_rms(wide) * gain_attn).astype(BF)
    projected = dot(attn_input, qkv)
    proj_q = projected[:, :dh]
    proj_k = projected[:, dh : 2 * dh]
    squares = jnp.stack([jnp.sum(proj_q * proj_q, axis=1), jnp.sum(proj_k * proj_k, axis=1)])
    squares = lax.psum(squares, "head") / width
    inv_q = lax.rsqrt(squares[0] + EPS)[:, None]
    inv_k = lax.rsqrt(squares[1] + EPS)[:, None]
    frequency = ROPE_BASE ** (-2.0 * jnp.arange(HD // 2, dtype=F32) / HD)
    angles = jnp.arange(seq, dtype=F32)[:, None] * frequency[None, :]
    cosine = jnp.cos(angles)[:, None, :]
    sine = jnp.sin(angles)[:, None, :]
    queries = rotate(proj_q * inv_q * gains_q, cosine, sine).astype(BF)
    keys = rotate(proj_k * inv_k * gains_k, cosine, sine).astype(BF)
    values = projected[:, 2 * dh :].astype(BF)
    valid = jnp.arange(seq, dtype=jnp.int32) < lengths[0]

    def probs_of(q, k):
        scores = jnp.where(valid[None, :], dot(q, k, NT) * scale, NEGATIVE)
        exponent = jnp.exp(scores - jnp.max(scores, axis=-1, keepdims=True))
        return exponent / jnp.sum(exponent, axis=-1, keepdims=True)

    attended = []
    for head in range(lh):
        part = slice(head * HD, (head + 1) * HD)
        probabilities = probs_of(queries[:, part], keys[:, part]).astype(BF)
        attended.append(dot(probabilities, values[:, part]).astype(BF))
    attended = jnp.concatenate(attended, axis=1)
    attended_all = gather_ring(attended).transpose(1, 0, 2).reshape(seq, width)
    residual = wide + dot(attended_all, full_out)
    inv_ffn = inverse_rms(residual)
    ffn_input = (residual * inv_ffn * gain_ffn).astype(BF)
    logits = dot(ffn_input, router)
    matches = info[:, :TOP, None] == jnp.arange(experts, dtype=jnp.int32)[None, None, :]
    chosen = (
        jnp.sum(jnp.where(matches, logits[:, None, :], 0.0), axis=-1)
        + info[:, TOP:].astype(F32) / 1024.0
    )
    chosen = jnp.exp(chosen - jnp.max(chosen, axis=1, keepdims=True))
    gates = chosen / jnp.sum(chosen, axis=1, keepdims=True)
    spread = jnp.sum(jnp.where(matches, gates[:, :, None], 0.0), axis=1)
    mine = lax.dynamic_slice_in_dim(spread, me * EXP_DEV, EXP_DEV, 1)
    cot_all = gather_ring(cotangent[0]).reshape(seq, width)
    mixed = jnp.zeros((seq, width), F32)
    grad_in = jnp.zeros((seq, width), F32)
    gate_dots, gate_grads, up_grads, down_grads = ([], [], [], [])
    for e in range(EXP_DEV):
        gate = mine[:, e : e + 1]
        gate_pre = dot(ffn_input, full_gate[e])
        up_pre = dot(ffn_input, full_up[e])
        sig = jax.nn.sigmoid(gate_pre)
        silu = gate_pre * sig
        act = (silu * up_pre).astype(BF)
        produced = dot(act, full_down[e]).astype(BF).astype(F32)
        mixed = mixed + gate * produced
        cot_f = cot_all.astype(F32)
        gate_dots.append(jnp.sum(produced * cot_f, axis=1))
        grad_out = (gate * cot_f).astype(BF)
        grad_act = dot(grad_out, full_down[e], NT)
        grad_gate_pre = (grad_act * up_pre * sig * (1.0 + gate_pre * (1.0 - sig))).astype(BF)
        grad_up_pre = (grad_act * silu).astype(BF)
        down_grads.append(dot(act, grad_out, TN).astype(BF))
        gate_grads.append(dot(ffn_input, grad_gate_pre, TN).astype(BF))
        up_grads.append(dot(ffn_input, grad_up_pre, TN).astype(BF))
        grad_in = grad_in + dot(grad_gate_pre, full_gate[e], NT) + dot(grad_up_pre, full_up[e], NT)
    grad_ffn = scatter_ring(grad_in.astype(BF).reshape(n, rows, width))
    summed = scatter_ring(mixed.astype(BF).reshape(n, rows, width))

    def over_fsdp(grads):
        return lax.psum_scatter(jnp.stack(grads), "fsdp", scatter_dimension=1, tiled=True).astype(
            F32
        )

    grad_w_gate = over_fsdp(gate_grads)
    grad_w_up = over_fsdp(up_grads)
    grad_w_down = over_fsdp(down_grads)
    dots = jnp.stack(gate_dots).reshape(EXP_DEV, n, rows).transpose(1, 0, 2)
    dots = lax.all_to_all(dots, "head", split_axis=0, concat_axis=0, tiled=True)
    dots = dots.reshape(experts, rows).T
    own_spread = own(spread)
    own_residual = own(residual)
    out_rows = own_residual + summed
    grad_rows = cotangent[0].astype(F32)
    grad_logits = own_spread * (dots - jnp.sum(own_spread * dots, axis=1, keepdims=True))
    high = lax.Precision.HIGHEST
    grad_ffn = grad_ffn + jnp.dot(grad_logits, router.astype(F32).T, precision=high)
    grad_router = jnp.dot(own(ffn_input).astype(F32).T, grad_logits, precision=high)

    def norm_back(values, gain, grad):
        inv = inverse_rms(values)
        unit = values * inv
        scaled = grad * gain
        back = inv * (scaled - unit * jnp.mean(scaled * unit, axis=-1, keepdims=True))
        return (back, jnp.sum(grad * unit, axis=0))

    back, grad_gain_ffn = norm_back(own_residual, gain_ffn, grad_ffn)
    grad_residual = grad_rows + back
    grad_attn_out = grad_residual.astype(BF)
    grad_attended = dot(grad_attn_out, full_out, NT).astype(BF)
    grad_heads = lax.all_to_all(
        grad_attended.reshape(rows, n, dh), "head", split_axis=1, concat_axis=0, tiled=True
    ).reshape(seq, dh)
    grad_q, grad_k, grad_v = ([], [], [])
    for head in range(lh):
        part = slice(head * HD, (head + 1) * HD)
        probabilities = probs_of(queries[:, part], keys[:, part])
        grad_probs = dot(grad_heads[:, part], values[:, part], NT)
        inner = jnp.sum(probabilities * grad_probs, axis=-1, keepdims=True)
        grad_scores = (probabilities * (grad_probs - inner)).astype(BF)
        grad_q.append((dot(grad_scores, keys[:, part]) * scale).astype(BF))
        grad_k.append((dot(grad_scores, queries[:, part], TN) * scale).astype(BF))
        grad_v.append(dot(probabilities.astype(BF), grad_heads[:, part], TN).astype(BF))
    turned_q = rotate(jnp.concatenate(grad_q, axis=1).astype(F32), cosine, -sine)
    turned_k = rotate(jnp.concatenate(grad_k, axis=1).astype(F32), cosine, -sine)
    unit_q = proj_q * inv_q
    unit_k = proj_k * inv_k
    means = jnp.stack(
        [jnp.sum(turned_q * gains_q * unit_q, axis=1), jnp.sum(turned_k * gains_k * unit_k, axis=1)]
    )
    means = lax.psum(means, "head") / width
    grad_projected = jnp.concatenate(
        [
            (inv_q * (turned_q * gains_q - unit_q * means[0][:, None])).astype(BF),
            (inv_k * (turned_k * gains_k - unit_k * means[1][:, None])).astype(BF),
            jnp.concatenate(grad_v, axis=1),
        ],
        axis=1,
    )
    grad_gain_q = jnp.sum(turned_q * unit_q, axis=0)
    grad_gain_k = jnp.sum(turned_k * unit_k, axis=0)
    grad_attn_in = dot(grad_projected, qkv, NT).astype(BF)
    grad_attn_in = scatter_ring(grad_attn_in.reshape(n, rows, width))
    grad_qkv = dot(attn_input, grad_projected, TN).astype(BF).reshape(n, m * shard, 3 * dh)
    grad_qkv = lax.psum_scatter(grad_qkv, "fsdp", scatter_dimension=1, tiled=True)
    grad_qkv = lax.all_to_all(grad_qkv, "head", split_axis=0, concat_axis=0, tiled=True)
    grad_qkv = grad_qkv.reshape(n, shard, 3, dh).transpose(1, 2, 0, 3).reshape(shard, 3 * width)
    grad_all = gather_ring(grad_attn_out).reshape(seq, width)
    grad_out_w = dot(attended, grad_all, TN)
    grad_out_w = lax.psum_scatter(grad_out_w, "fsdp", scatter_dimension=0, tiled=True)
    back, grad_gain_attn = norm_back(hidden[0].astype(F32), gain_attn, grad_attn_in)
    grad_hidden = grad_residual + back

    def at_mine(piece):
        return lax.dynamic_update_slice_in_dim(jnp.zeros((width,), F32), piece, me * dh, 0)[:, None]

    pack = jnp.concatenate(
        [
            grad_router,
            grad_gain_attn[:, None],
            grad_gain_ffn[:, None],
            at_mine(grad_gain_q),
            at_mine(grad_gain_k),
        ],
        axis=1,
    ).reshape(n * m, shard * (experts + 4))
    pack = lax.all_to_all(pack, both, split_axis=0, concat_axis=0, tiled=True)
    pack = jnp.sum(pack, axis=0).reshape(shard, experts + 4)
    return (
        out_rows.astype(BF)[None],
        grad_hidden[None],
        grad_qkv.astype(F32),
        grad_out_w,
        pack[:, :experts],
        pack[:, experts],
        pack[:, experts + 1],
        pack[:, experts + 2],
        pack[:, experts + 3],
        grad_w_gate,
        grad_w_up,
        grad_w_down,
    )


def solution(mesh):
    both = ("head", "fsdp")
    return jax.shard_map(
        body,
        mesh=mesh,
        in_specs=(
            P("fsdp", "head", None),
            P(both, None),
            P(both, None),
            P(both, None),
            P(both),
            P(both),
            P(both),
            P(both),
            P("head", "fsdp", None),
            P("head", "fsdp", None),
            P("head", "fsdp", None),
            P("fsdp"),
            P("fsdp", "head", None),
            P("fsdp", "head", None),
            P("fsdp", "head", None),
        ),
        out_specs=(
            P("fsdp", "head", None),
            P("fsdp", "head", None),
            P(both, None),
            P(both, None),
            P(both, None),
            P(both),
            P(both),
            P(both),
            P(both),
            P("head", "fsdp", None),
            P("head", "fsdp", None),
            P("head", "fsdp", None),
        ),
        check_vma=False,
    )
```

profile of v0, /device:TPU:0, one launch (start us, length us, event | category | flops | bytes accessed | tf_op | source)
XLA Modules:
  0.0 871.2 jit_solution(12422500406623019625)
XLA Ops:
  10.0 27.5 %all_to_all.40 = bf16[8,64,768]{2,1,0:T(8,128)(2,1)} all-to-all(bf16[8,64,768]{2,1,0:T(8,128)(2,1)S(1)} %reshape.375), channel_id=1, replica_groups=mesh['head'=8,'fsdp'=4] {'head'}, dimensions={0} | all-to-all | bytes 1572864 | tf_op jit(solution)/shard_map/all_to_all | solution.py:149
  45.0 53.5 %all-gather = bf16[32,64,20]{1,2,0:T(8,128)(2,1)S(1)} all-gather(bf16[1,64,20]{1,2,0:T(8,128)(2,1)S(1)} %bitcast.496), channel_id=1, replica_groups=mesh['head'=8,'fsdp'=4] {'head','fsdp'}, dimensions={0}, use_global_device_ids=true | all-gather | bytes 84480 | tf_op jit(solution)/shard_map/all_gather | solution.py:142
  127.1 25.3 %collective-permute-done.33 = bf16[128,2048]{1,0:T(8,128)(2,1)} collective-permute-done((bf16[128,2048]{1,0:T(8,128)(2,1)S(1)}, bf16[128,2048]{1,0:T(8,128)(2,1)}, u32[]{:S(2)}, u32[]{:S(2)}) %collective-permute-start.33) | collective-permute-done | bytes 524320 | tf_op jit(solution)/shard_map/ppermute | solution.py:57
  157.2 7.3 collective-permute-done.3
  167.3 8.4 collective-permute-done.35
  179.5 7.4 collective-permute-done.5
  190.6 7.6 collective-permute-done.37
  213.6 7.9 fusion.132
  221.7 20.3 %psum.14 = f32[2,1024]{1,0:T(2,128)} all-reduce(f32[2,1024]{1,0:T(2,128)S(1)} %pad_maximum_fusion.17), channel_id=1, replica_groups=mesh['head'=8,'fsdp'=4] {'head'}, use_global_device_ids=true, to_apply=%region_3.4 | all-reduce | flops 2048 | bytes 16384 | tf_op jit(solution)/shard_map/psum | solution.py:170
  258.6 10.1 %collective-permute-done.8 = bf16[1024,256]{0,1:T(8,128)(2,1)S(1)} collective-permute-done((bf16[1024,256]{0,1:T(8,128)(2,1)S(1)}, bf16[1024,256]{0,1:T(8,128)(2,1)S(1)}, u32[]{:S(2)}, u32[]{:S(2)}) %collective-permute-start.8) | collective-permute-done | bytes 524320 | tf_op jit(solution)/shard_map/ppermute | solution.py:56
  277.1 6.1 collective-permute-done.10
  288.2 6.6 collective-permute-done.12
  302.5 14.3 %multiply_reduce_fusion = (f32[1024]{0:T(1024)S(1)}, f32[1024,2048]{1,0:T(8,128)S(1)}) fusion(bf16[1024,2048]{0,1:T(8,128)(2,1)} %bitcast.38, bf16[2048,2048]{1,0:T(8,128)(2,1)} %all-gather.9.cloned.1.call-done, bf16[8,128,2048]{2,1,0:T(8,128)(2,1)} %fusion.75), kind=kOutput, calls=%fused_computation.30 | convolution fusion | flops 8598322176 | bytes 25169920 | tf_op jit(solution)/shard_map/dot_general | solution.py:103
  329.3 10.0 %fusion.18 = f32[1024,1024]{1,0:T(8,128)} fusion(bf16[1024,2048]{1,0:T(8,128)(2,1)} %copy-done.6, bf16[2,2048,1024]{2,1,0:T(8,128)(2,1)} %all-gather.11.cloned.1.call-done), kind=kOutput, calls=%fused_computation.67 | convolution fusion | flops 4294967296 | bytes 12582912 | tf_op jit(solution)/shard_map/dot_general | solution.py:103
  339.3 6.5 fusion.23
  345.8 10.0 %fusion.20 = f32[1024,1024]{1,0:T(8,128)} fusion(bf16[1024,2048]{1,0:T(8,128)(2,1)} %copy-done.6, bf16[2,2048,1024]{2,1,0:T(8,128)(2,1)} %all-gather.13.cloned.1.call-done), kind=kOutput, calls=%fused_computation.69 | convolution fusion | flops 4294967296 | bytes 12582912 | tf_op jit(solution)/shard_map/dot_general | solution.py:103
  355.9 6.1 fusion.24
  362.0 12.2 %multiply_convert_fusion.5 = (bf16[1024,1024]{1,0:T(8,128)(2,1)S(1)}, bf16[1024,1024]{1,0:T(8,128)(2,1)S(1)}, bf16[1024,1024]{1,0:T(8,128)(2,1)}) fusion(f32[1024,1024]{1,0:T(8,128)} %fusion.18, f32[1024,1024]{1,0:T(8,128)} %fusion.20, bf16[1024,2048]{1,0:T(8,128)(2,1)} %bitcast.454, bf16[2,1024,2048]{2,1,0:T(8,128)(2,1)} %all-gather.15.cloned.1.call-done), kind=kOutput, calls=%fused_computation.49 | convolution fusion | flops 4310695936 | bytes 23068672 | tf_op jit(solution)/shard_map/dot_general | solution.py:103
  374.2 10.4 %fusion.17 = f32[1024,2048]{1,0:T(8,128)} fusion(bf16[1024,1024]{1,0:T(8,128)(2,1)S(1)} %get-tuple-element.89, bf16[2,2048,1024]{2,1,0:T(8,128)(2,1)} %all-gather.11.cloned.1.call-done), kind=kOutput, calls=%fused_computation.66 | convolution fusion | flops 4294967296 | bytes 14680064 | tf_op jit(solution)/shard_map/dot_general | solution.py:103
  384.7 9.1 %fusion.19 = f32[1024,2048]{1,0:T(8,128)} fusion(bf16[1024,1024]{1,0:T(8,128)(2,1)S(1)} %get-tuple-element.88, bf16[2,2048,1024]{2,1,0:T(8,128)(2,1)} %all-gather.13.cloned.1.call-done), kind=kOutput, calls=%fused_computation.68 | convolution fusion | flops 4294967296 | bytes 14680064 | tf_op jit(solution)/shard_map/dot_general | solution.py:103
  393.8 10.4 %multiply_convert_fusion.3 = (bf16[1024,1024]{1,0:T(8,128)(2,1)S(1)}, bf16[1024,1024]{1,0:T(8,128)(2,1)}, bf16[1024,1024]{1,0:T(8,128)(2,1)}) fusion(f32[1024,1024]{1,0:T(8,128)} %fusion.23, f32[1024,1024]{1,0:T(8,128)} %fusion.24, bf16[1024,2048]{1,0:T(8,128)(2,1)S(1)} %bitcast.453, bf16[2,1024,2048]{2,1,0:T(8,128)(2,1)S(1)} %bitcast.530), kind=kOutput, calls=%fused_computation.47 | convolution fusion | flops 4310695936 | bytes 23068672 | tf_op jit(solution)/shard_map/dot_general | solution.py:103
  404.2 9.1 %fusion.22 = f32[1024,2048]{1,0:T(8,128)} fusion(bf16[1024,1024]{1,0:T(8,128)(2,1)} %get-tuple-element.86, bf16[2,2048,1024]{2,1,0:T(8,128)(2,1)S(1)} %bitcast.532), kind=kOutput, calls=%fused_computation.71 | convolution fusion | flops 4294967296 | bytes 14680064 | tf_op jit(solution)/shard_map/dot_general | solution.py:103
  413.4 13.3 %add_convert_fusion = bf16[1024,2048]{1,0:T(8,128)(2,1)} fusion(f32[1024,2048]{1,0:T(8,128)} %fusion.22, f32[1024,2048]{1,0:T(8,128)} %fusion.17, f32[1024,2048]{1,0:T(8,128)} %fusion.19, bf16[1024,1024]{1,0:T(8,128)(2,1)S(1)} %get-tuple-element.85, bf16[2,2048,1024]{2,1,0:T(8,128)(2,1)} %all-gather.13.cloned.1.call-done), kind=kOutput, calls=%fused_computation.28 | convolution fusion | flops 4303355904 | bytes 35651584 | tf_op jit(solution)/shard_map/dot_general | solution.py:103
  430.1 6.9 collective-permute-done.40
  440.5 11.3 %collective-permute-done.41 = bf16[128,2048]{1,0:T(8,128)(2,1)S(1)} collective-permute-done((bf16[128,2048]{1,0:T(8,128)(2,1)S(1)}, bf16[128,2048]{1,0:T(8,128)(2,1)S(1)}, u32[]{:S(2)}, u32[]{:S(2)}) %collective-permute-start.41) | collective-permute-done | bytes 524320 | tf_op jit(solution)/shard_map/ppermute | solution.py:86
  453.3 7.5 convolution_convert_fusion.1
  465.8 12.6 %fusion.2 = (f32[1024]{0:T(1024)S(1)}, f32[1024]{0:T(1024)S(1)}, bf16[1024,2048]{1,0:T(8,128)(2,1)}, bf16[1024,2048]{1,0:T(8,128)(2,1)}, bf16[1024,2048]{1,0:T(8,128)(2,1)}) fusion(bf16[8,128,2048]{2,1,0:T(8,128)(2,1)} %fusion.77, bf16[1024,2048]{1,0:T(8,128)(2,1)S(1)} %convolution_convert_fusion.1, f32[1024]{0:T(1024)S(1)} %bitcast.500, ...), kind=kOutput, calls=%fused_computation.6 | convolution fusion | flops 4328519680 | bytes 27279360 | tf_op jit(solution)/shard_map/dot_general | solution.py:103
  502.5 6.5 convolution_convert_fusion.4
  542.8 19.8 %psum.15 = f32[2,1024]{1,0:T(2,128)S(1)} all-reduce(f32[2,1024]{1,0:T(2,128)S(1)} %pad_maximum_fusion.18), channel_id=1, replica_groups=mesh['head'=8,'fsdp'=4] {'head'}, use_global_device_ids=true, to_apply=%region_23.24 | all-reduce | flops 2048 | bytes 16384 | tf_op jit(solution)/shard_map/psum | solution.py:284
  570.6 7.6 convert_bitcast_fusion.1
  578.3 6.2 convert_bitcast_fusion
  584.5 6.3 pad_maximum_fusion.2
  590.9 7.6 convert_bitcast_fusion.3
  598.6 6.3 convert_bitcast_fusion.2
  604.9 6.3 pad_maximum_fusion.1
  613.1 7.7 convert_bitcast_fusion.5
  620.8 6.2 convert_bitcast_fusion.4
  627.0 6.2 pad_maximum_fusion
  647.4 7.6 collective-permute-done.56
  657.2 5.7 convolution_convert_fusion
  663.5 11.3 %collective-permute-done.58 = bf16[128,2048]{1,0:T(8,128)(2,1)S(1)} collective-permute-done((bf16[128,2048]{1,0:T(8,128)(2,1)S(1)}, bf16[128,2048]{1,0:T(8,128)(2,1)S(1)}, u32[]{:S(2)}, u32[]{:S(2)}) %collective-permute-start.58) | collective-permute-done | bytes 524320 | tf_op jit(solution)/shard_map/ppermute | solution.py:56
  681.4 7.4 collective-permute-done.60
  691.8 8.3 collective-permute-done.49
  712.0 5.7 collective-permute-done.50
  747.6 6.8 all-to-all-done.4
  762.2 23.2 %collective-permute-done.31 = bf16[128,2048]{1,0:T(8,128)(2,1)S(1)} collective-permute-done((bf16[128,2048]{1,0:T(8,128)(2,1)S(1)}, bf16[128,2048]{1,0:T(8,128)(2,1)S(1)}, u32[]{:S(2)}, u32[]{:S(2)}) %collective-permute-start.31) | collective-permute-done | bytes 524320 | tf_op jit(solution)/shard_map/ppermute | solution.py:87
  802.9 26.6 %reduce-scatter.10.cloned.1.call-done = bf16[2,512,1024]{2,1,0:T(8,128)(2,1)} async-done(((bf16[2,2048,1024]{2,1,0:T(8,128)(2,1)}), bf16[2,512,1024]{2,1,0:T(8,128)(2,1)}) %reduce-scatter.10.cloned.1.call-update) | async-done | bytes 2097168 | tf_op jit(solution)/shard_map/reduce_scatter | solution.py:234
  833.5 30.4 %reduce-scatter.8.cloned.1.call-done = f32[64,2048]{1,0:T(8,128)} async-done(((f32[256,2048]{1,0:T(8,128)}), f32[64,2048]{1,0:T(8,128)}) %reduce-scatter.8.cloned.1.call-update) | async-done | bytes 524304 | tf_op jit(solution)/shard_map/reduce_scatter | solution.py:303
  (511 shorter events, 296.6 us)
Async XLA Ops:
  7.2 206.4 %all-gather.7.cloned.1.call-start = ((), (), s32[]{:S(2)}) async-start(), calls=%async_computation.10 | async-start | bytes 3932160 | tf_op jit(solution)/shard_map/all_gather | solution.py:150
  37.5 265.0 %all-gather.9.cloned.1.call-start = ((), (), s32[]{:S(2)}) async-start(), calls=%async_computation.11 | async-start | bytes 8650752 | tf_op jit(solution)/shard_map/all_gather | solution.py:153
  38.2 291.1 %all-gather.11.cloned.1.call-start = ((), (), s32[]{:S(2)}) async-start(), calls=%async_computation.12 | async-start | bytes 10485760 | tf_op jit(solution)/shard_map/all_gather | solution.py:154
  39.0 306.8 %all-gather.13.cloned.1.call-start = ((), (), s32[]{:S(2)}) async-start(), calls=%async_computation.13 | async-start | bytes 10485760 | tf_op jit(solution)/shard_map/all_gather | solution.py:155
  39.5 322.5 %all-gather.15.cloned.1.call-start = ((), (), s32[]{:S(2)}) async-start(), calls=%async_computation.14 | async-start | bytes 10485760 | tf_op jit(solution)/shard_map/all_gather | solution.py:156
  39.6 69.0 %collective-permute-start.16 = (s32[128,16]{0,1:T(8,128)S(1)}, s32[128,16]{0,1:T(8,128)S(1)}, u32[]{:S(2)}, u32[]{:S(2)}) collective-permute-start(s32[128,16]{0,1:T(8,128)S(1)} %pad_add_fusion), channel_id=1, source_target_pairs={{0,8},{8,16},{16,24},{24,28},{28,20},{20,12},{12,4},{4,0},{1,9},{9... | collective-permute-start | bytes 24584 | tf_op jit(solution)/shard_map/ppermute | solution.py:56
  40.8 67.9 %collective-permute-start.17 = (s32[128,16]{0,1:T(8,128)S(1)}, s32[128,16]{0,1:T(8,128)S(1)}, u32[]{:S(2)}, u32[]{:S(2)}) collective-permute-start(s32[128,16]{0,1:T(8,128)S(1)} %pad_add_fusion), channel_id=1, source_target_pairs={{8,0},{16,8},{24,16},{28,24},{20,28},{12,20},{4,12},{0,4},{9,1},{1... | collective-permute-start | bytes 24584 | tf_op jit(solution)/shard_map/ppermute | solution.py:57
  41.7 80.4 %collective-permute-start = (bf16[128,2048]{1,0:T(8,128)(2,1)S(1)}, bf16[128,2048]{1,0:T(8,128)(2,1)S(1)}, u32[]{:S(2)}, u32[]{:S(2)}) collective-permute-start(bf16[128,2048]{1,0:T(8,128)(2,1)S(1)} %bitcast.420), channel_id=1, source_target_pairs={{0,8},{8,16},{16,24},{24,28},{28,20},{20,12},{12,4},{4,0},{1,9},{9... | collective-permute-start | bytes 1572872 | tf_op jit(solution)/shard_map/ppermute | solution.py:56
  42.8 80.6 %collective-permute-start.1 = (bf16[128,2048]{1,0:T(8,128)(2,1)S(1)}, bf16[128,2048]{1,0:T(8,128)(2,1)S(1)}, u32[]{:S(2)}, u32[]{:S(2)}) collective-permute-start(bf16[128,2048]{1,0:T(8,128)(2,1)S(1)} %bitcast.421), channel_id=1, source_target_pairs={{8,0},{16,8},{24,16},{28,24},{20,28},{12,20},{4,12},{0,4},{9,1},{1... | collective-permute-start | bytes 1572872 | tf_op jit(solution)/shard_map/ppermute | solution.py:57
  43.7 82.2 %collective-permute-start.32 = (bf16[128,2048]{1,0:T(8,128)(2,1)S(1)}, bf16[128,2048]{1,0:T(8,128)(2,1)S(1)}, u32[]{:S(2)}, u32[]{:S(2)}) collective-permute-start(bf16[128,2048]{1,0:T(8,128)(2,1)S(1)} %bitcast.434), channel_id=1, source_target_pairs={{0,8},{8,16},{16,24},{24,28},{28,20},{20,12},{12,4},{4,0},{1,9},{9... | collective-permute-start | bytes 1572872 | tf_op jit(solution)/shard_map/ppermute | solution.py:56
  120.3 32.1 %collective-permute-start.33 = (bf16[128,2048]{1,0:T(8,128)(2,1)S(1)}, bf16[128,2048]{1,0:T(8,128)(2,1)}, u32[]{:S(2)}, u32[]{:S(2)}) collective-permute-start(bf16[128,2048]{1,0:T(8,128)(2,1)S(1)} %bitcast.435), channel_id=1, source_target_pairs={{8,0},{16,8},{24,16},{28,24},{20,28},{12,20},{4,12},{0,4},{9,1},{1... | collective-permute-start | bytes 1572872 | tf_op jit(solution)/shard_map/ppermute | solution.py:57
  122.2 32.2 %collective-permute-start.2 = (bf16[128,2048]{1,0:T(8,128)(2,1)S(1)}, bf16[128,2048]{1,0:T(8,128)(2,1)S(1)}, u32[]{:S(2)}, u32[]{:S(2)}) collective-permute-start(bf16[128,2048]{1,0:T(8,128)(2,1)S(1)} %collective-permute-done), channel_id=1, source_target_pairs={{0,8},{8,16},{16,24},{24,28},{28,20},{20,12},{12,4},{4,0},{1,9},{9... | collective-permute-start | bytes 1572872 | tf_op jit(solution)/shard_map/ppermute | solution.py:56
  123.4 41.0 %collective-permute-start.3 = (bf16[128,2048]{1,0:T(8,128)(2,1)S(1)}, bf16[128,2048]{1,0:T(8,128)(2,1)S(1)}, u32[]{:S(2)}, u32[]{:S(2)}) collective-permute-start(bf16[128,2048]{1,0:T(8,128)(2,1)S(1)} %collective-permute-done.1), channel_id=1, source_target_pairs={{8,0},{16,8},{24,16},{28,24},{20,28},{12,20},{4,12},{0,4},{9,1},{1... | collective-permute-start | bytes 1572872 | tf_op jit(solution)/shard_map/ppermute | solution.py:57
  125.9 38.7 %collective-permute-start.34 = (bf16[128,2048]{1,0:T(8,128)(2,1)S(1)}, bf16[128,2048]{1,0:T(8,128)(2,1)S(1)}, u32[]{:S(2)}, u32[]{:S(2)}) collective-permute-start(bf16[128,2048]{1,0:T(8,128)(2,1)S(1)} %collective-permute-done.32), channel_id=1, source_target_pairs={{0,8},{8,16},{16,24},{24,28},{28,20},{20,12},{12,4},{4,0},{1,9},{9... | collective-permute-start | bytes 1572872 | tf_op jit(solution)/shard_map/ppermute | solution.py:56
  152.4 23.3 %collective-permute-start.35 = (bf16[128,2048]{1,0:T(8,128)(2,1)}, bf16[128,2048]{1,0:T(8,128)(2,1)S(1)}, u32[]{:S(2)}, u32[]{:S(2)}) collective-permute-start(bf16[128,2048]{1,0:T(8,128)(2,1)} %collective-permute-done.33), channel_id=1, source_target_pairs={{8,0},{16,8},{24,16},{28,24},{20,28},{12,20},{4,12},{0,4},{9,1},{1... | collective-permute-start | bytes 1572872 | tf_op jit(solution)/shard_map/ppermute | solution.py:57
  154.3 23.2 %collective-permute-start.4 = (bf16[128,2048]{1,0:T(8,128)(2,1)S(1)}, bf16[128,2048]{1,0:T(8,128)(2,1)S(1)}, u32[]{:S(2)}, u32[]{:S(2)}) collective-permute-start(bf16[128,2048]{1,0:T(8,128)(2,1)S(1)} %collective-permute-done.2), channel_id=1, source_target_pairs={{0,8},{8,16},{16,24},{24,28},{28,20},{20,12},{12,4},{4,0},{1,9},{9... | collective-permute-start | bytes 1572872 | tf_op jit(solution)/shard_map/ppermute | solution.py:56
  164.5 22.5 %collective-permute-start.5 = (bf16[128,2048]{1,0:T(8,128)(2,1)S(1)}, bf16[128,2048]{1,0:T(8,128)(2,1)S(1)}, u32[]{:S(2)}, u32[]{:S(2)}) collective-permute-start(bf16[128,2048]{1,0:T(8,128)(2,1)S(1)} %collective-permute-done.3), channel_id=1, source_target_pairs={{8,0},{16,8},{24,16},{28,24},{20,28},{12,20},{4,12},{0,4},{9,1},{1... | collective-permute-start | bytes 1572872 | tf_op jit(solution)/shard_map/ppermute | solution.py:57
  164.6 22.5 %collective-permute-start.36 = (bf16[128,2048]{1,0:T(8,128)(2,1)S(1)}, bf16[128,2048]{1,0:T(8,128)(2,1)S(1)}, u32[]{:S(2)}, u32[]{:S(2)}) collective-permute-start(bf16[128,2048]{1,0:T(8,128)(2,1)S(1)} %collective-permute-done.34), channel_id=1, source_target_pairs={{0,8},{8,16},{16,24},{24,28},{28,20},{20,12},{12,4},{4,0},{1,9},{9... | collective-permute-start | bytes 1572872 | tf_op jit(solution)/shard_map/ppermute | solution.py:56
  175.7 22.5 %collective-permute-start.37 = (bf16[128,2048]{1,0:T(8,128)(2,1)S(1)}, bf16[128,2048]{1,0:T(8,128)(2,1)S(1)}, u32[]{:S(2)}, u32[]{:S(2)}) collective-permute-start(bf16[128,2048]{1,0:T(8,128)(2,1)S(1)} %collective-permute-done.35), channel_id=1, source_target_pairs={{8,0},{16,8},{24,16},{28,24},{20,28},{12,20},{4,12},{0,4},{9,1},{1... | collective-permute-start | bytes 1572872 | tf_op jit(solution)/shard_map/ppermute | solution.py:57
  177.6 24.3 %collective-permute-start.6 = (bf16[64,2048]{1,0:T(8,128)(2,1)S(1)}, bf16[64,2048]{1,0:T(8,128)(2,1)S(1)}, u32[]{:S(2)}, u32[]{:S(2)}) collective-permute-start(bf16[64,2048]{1,0:T(8,128)(2,1)S(1)} %slice.410), channel_id=1, source_target_pairs={{0,8},{8,16},{16,24},{24,28},{28,20},{20,12},{12,4},{4,0},{1,9},{9... | collective-permute-start | bytes 786440 | tf_op jit(solution)/shard_map/ppermute | solution.py:60
  187.0 16.8 %collective-permute-start.7 = (bf16[64,2048]{1,0:T(8,128)(2,1)S(1)}, bf16[64,2048]{1,0:T(8,128)(2,1)S(1)}, u32[]{:S(2)}, u32[]{:S(2)}) collective-permute-start(bf16[64,2048]{1,0:T(8,128)(2,1)S(1)} %slice.411), channel_id=1, source_target_pairs={{8,0},{16,8},{24,16},{28,24},{20,28},{12,20},{4,12},{0,4},{9,1},{1... | collective-permute-start | bytes 786440 | tf_op jit(solution)/shard_map/ppermute | solution.py:61
  188.6 82.4 %collective-permute-start.38 = (bf16[64,2048]{1,0:T(8,128)(2,1)}, bf16[64,2048]{1,0:T(8,128)(2,1)}, u32[]{:S(2)}, u32[]{:S(2)}) collective-permute-start(bf16[64,2048]{1,0:T(8,128)(2,1)} %slice.443), channel_id=1, source_target_pairs={{0,8},{8,16},{16,24},{24,28},{28,20},{20,12},{12,4},{4,0},{1,9},{9... | collective-permute-start | bytes 786440 | tf_op jit(solution)/shard_map/ppermute | solution.py:60
  199.7 71.3 %collective-permute-start.39 = (bf16[64,2048]{1,0:T(8,128)(2,1)}, bf16[64,2048]{1,0:T(8,128)(2,1)}, u32[]{:S(2)}, u32[]{:S(2)}) collective-permute-start(bf16[64,2048]{1,0:T(8,128)(2,1)} %slice.444), channel_id=1, source_target_pairs={{8,0},{16,8},{24,16},{28,24},{20,28},{12,20},{4,12},{0,4},{9,1},{1... | collective-permute-start | bytes 786440 | tf_op jit(solution)/shard_map/ppermute | solution.py:61
  254.6 14.0 %collective-permute-start.8 = (bf16[1024,256]{0,1:T(8,128)(2,1)S(1)}, bf16[1024,256]{0,1:T(8,128)(2,1)S(1)}, u32[]{:S(2)}, u32[]{:S(2)}) collective-permute-start(bf16[1024,256]{0,1:T(8,128)(2,1)S(1)} %pad_maximum_fusion.8), channel_id=1, source_target_pairs={{0,8},{8,16},{16,24},{24,28},{28,20},{20,12},{12,4},{4,0},{1,9},{9... | collective-permute-start | bytes 1572872 | tf_op jit(solution)/shard_map/ppermute | solution.py:56
  268.7 14.6 %collective-permute-start.10 = (bf16[1024,256]{0,1:T(8,128)(2,1)S(1)}, bf16[1024,256]{0,1:T(8,128)(2,1)S(1)}, u32[]{:S(2)}, u32[]{:S(2)}) collective-permute-start(bf16[1024,256]{0,1:T(8,128)(2,1)S(1)} %collective-permute-done.8), channel_id=1, source_target_pairs={{0,8},{8,16},{16,24},{24,28},{28,20},{20,12},{12,4},{4,0},{1,9},{9... | collective-permute-start | bytes 1572872 | tf_op jit(solution)/shard_map/ppermute | solution.py:56
  268.8 14.6 %collective-permute-start.11 = (bf16[1024,256]{0,1:T(8,128)(2,1)S(1)}, bf16[1024,256]{0,1:T(8,128)(2,1)S(1)}, u32[]{:S(2)}, u32[]{:S(2)}) collective-permute-start(bf16[1024,256]{0,1:T(8,128)(2,1)S(1)} %collective-permute-done.9), channel_id=1, source_target_pairs={{8,0},{16,8},{24,16},{28,24},{20,28},{12,20},{4,12},{0,4},{9,1},{1... | collective-permute-start | bytes 1572872 | tf_op jit(solution)/shard_map/ppermute | solution.py:57
  438.6 22.2 %collective-permute-start.45 = (bf16[128,2048]{1,0:T(8,128)(2,1)S(1)}, bf16[128,2048]{1,0:T(8,128)(2,1)S(1)}, u32[]{:S(2)}, u32[]{:S(2)}) collective-permute-start(bf16[128,2048]{1,0:T(8,128)(2,1)S(1)} %pad_maximum_fusion.12), channel_id=1, source_target_pairs={{8,0},{16,8},{24,16},{28,24},{20,28},{12,20},{4,12},{0,4},{9,1},{1... | collective-permute-start | bytes 1572872 | tf_op jit(solution)/shard_map/ppermute | solution.py:87
  463.8 21.9 %collective-permute-start.46 = (bf16[128,2048]{1,0:T(8,128)(2,1)S(1)}, bf16[128,2048]{1,0:T(8,128)(2,1)S(1)}, u32[]{:S(2)}, u32[]{:S(2)}) collective-permute-start(bf16[128,2048]{1,0:T(8,128)(2,1)S(1)} %get-tuple-element.103), channel_id=1, source_target_pairs={{8,0},{16,8},{24,16},{28,24},{20,28},{12,20},{4,12},{0,4},{9,1},{1... | collective-permute-start | bytes 1572872 | tf_op jit(solution)/shard_map/ppermute | solution.py:87
  509.8 14.9 %all-to-all-start.2 = ((bf16[128,8,256]{2,0,1:T(8,128)(2,1)}), bf16[128,8,256]{2,0,1:T(8,128)(2,1)S(1)}, u32[]{:S(2)}, u32[]{:S(2)}) async-start(bf16[128,8,256]{2,0,1:T(8,128)(2,1)} %bitcast.414), calls=%async_computation.2 | async-start | bytes 1048576 | tf_op jit(solution)/shard_map/all_to_all | solution.py:264
  514.4 240.0 %reduce-scatter.6.cloned.1.call-start = ((), (), s32[]{:S(2)}) async-start(), calls=%async_computation.15 | async-start | bytes 3932160 | tf_op jit(solution)/shard_map/reduce_scatter | solution.py:298
  570.4 224.3 %reduce-scatter.14.cloned.1.call-start = ((), (), s32[]{:S(2)}) async-start(), calls=%async_computation.19 | async-start | bytes 10485760 | tf_op jit(solution)/shard_map/reduce_scatter | solution.py:234
  590.8 208.0 %reduce-scatter.12.cloned.1.call-start = ((), (), s32[]{:S(2)}) async-start(), calls=%async_computation.18 | async-start | bytes 10485760 | tf_op jit(solution)/shard_map/reduce_scatter | solution.py:234
  611.2 218.3 %reduce-scatter.10.cloned.1.call-start = ((), (), s32[]{:S(2)}) async-start(), calls=%async_computation.17 | async-start | bytes 10485760 | tf_op jit(solution)/shard_map/reduce_scatter | solution.py:234
  633.2 230.7 %reduce-scatter.8.cloned.1.call-start = ((), (), s32[]{:S(2)}) async-start(), calls=%async_computation.16 | async-start | bytes 2621440 | tf_op jit(solution)/shard_map/reduce_scatter | solution.py:303
  637.0 18.0 %collective-permute-start.56 = (bf16[128,2048]{1,0:T(8,128)(2,1)S(1)}, bf16[128,2048]{1,0:T(8,128)(2,1)S(1)}, u32[]{:S(2)}, u32[]{:S(2)}) collective-permute-start(bf16[128,2048]{1,0:T(8,128)(2,1)S(1)} %copy-done.37), channel_id=1, source_target_pairs={{0,8},{8,16},{16,24},{24,28},{28,20},{20,12},{12,4},{4,0},{1,9},{9... | collective-permute-start | bytes 1572872 | tf_op jit(solution)/shard_map/ppermute | solution.py:56
  637.1 18.1 %collective-permute-start.57 = (bf16[128,2048]{1,0:T(8,128)(2,1)S(1)}, bf16[128,2048]{1,0:T(8,128)(2,1)S(1)}, u32[]{:S(2)}, u32[]{:S(2)}) collective-permute-start(bf16[128,2048]{1,0:T(8,128)(2,1)S(1)} %copy-done.37), channel_id=1, source_target_pairs={{8,0},{16,8},{24,16},{28,24},{20,28},{12,20},{4,12},{0,4},{9,1},{1... | collective-permute-start | bytes 1572872 | tf_op jit(solution)/shard_map/ppermute | solution.py:57
  645.2 85.1 %collective-permute-start.29 = (bf16[128,2048]{1,0:T(8,128)(2,1)S(1)}, bf16[128,2048]{1,0:T(8,128)(2,1)}, u32[]{:S(2)}, u32[]{:S(2)}) collective-permute-start(bf16[128,2048]{1,0:T(8,128)(2,1)S(1)} %pad_maximum_fusion.10), channel_id=1, source_target_pairs={{8,0},{16,8},{24,16},{28,24},{20,28},{12,20},{4,12},{0,4},{9,1},{1... | collective-permute-start | bytes 1572872 | tf_op jit(solution)/shard_map/ppermute | solution.py:87
  645.4 74.5 %collective-permute-start.25 = (bf16[128,2048]{1,0:T(8,128)(2,1)S(1)}, bf16[128,2048]{1,0:T(8,128)(2,1)S(1)}, u32[]{:S(2)}, u32[]{:S(2)}) collective-permute-start(bf16[128,2048]{1,0:T(8,128)(2,1)S(1)} %pad_maximum_fusion.9), channel_id=1, source_target_pairs={{0,8},{8,16},{16,24},{24,28},{28,20},{20,12},{12,4},{4,0},{1,9},{9... | collective-permute-start | bytes 1572872 | tf_op jit(solution)/shard_map/ppermute | solution.py:86
  655.1 19.7 %collective-permute-start.58 = (bf16[128,2048]{1,0:T(8,128)(2,1)S(1)}, bf16[128,2048]{1,0:T(8,128)(2,1)S(1)}, u32[]{:S(2)}, u32[]{:S(2)}) collective-permute-start(bf16[128,2048]{1,0:T(8,128)(2,1)S(1)} %collective-permute-done.56), channel_id=1, source_target_pairs={{0,8},{8,16},{16,24},{24,28},{28,20},{20,12},{12,4},{4,0},{1,9},{9... | collective-permute-start | bytes 1572872 | tf_op jit(solution)/shard_map/ppermute | solution.py:56
  655.3 19.5 %collective-permute-start.59 = (bf16[128,2048]{1,0:T(8,128)(2,1)S(1)}, bf16[128,2048]{1,0:T(8,128)(2,1)S(1)}, u32[]{:S(2)}, u32[]{:S(2)}) collective-permute-start(bf16[128,2048]{1,0:T(8,128)(2,1)S(1)} %collective-permute-done.57), channel_id=1, source_target_pairs={{8,0},{16,8},{24,16},{28,24},{20,28},{12,20},{4,12},{0,4},{9,1},{1... | collective-permute-start | bytes 1572872 | tf_op jit(solution)/shard_map/ppermute | solution.py:57
  663.0 14.6 %collective-permute-start.48 = (bf16[64,2048]{1,0:T(8,128)(2,1)S(1)}, bf16[64,2048]{1,0:T(8,128)(2,1)S(1)}, u32[]{:S(2)}, u32[]{:S(2)}) collective-permute-start(bf16[64,2048]{1,0:T(8,128)(2,1)S(1)} %get-tuple-element.98), channel_id=1, source_target_pairs={{0,8},{8,16},{16,24},{24,28},{28,20},{20,12},{12,4},{4,0},{1,9},{9... | collective-permute-start | bytes 786440 | tf_op jit(solution)/shard_map/ppermute | solution.py:75
  674.8 14.0 %collective-permute-start.60 = (bf16[128,2048]{1,0:T(8,128)(2,1)S(1)}, bf16[128,2048]{1,0:T(8,128)(2,1)S(1)}, u32[]{:S(2)}, u32[]{:S(2)}) collective-permute-start(bf16[128,2048]{1,0:T(8,128)(2,1)S(1)} %collective-permute-done.58), channel_id=1, source_target_pairs={{0,8},{8,16},{16,24},{24,28},{28,20},{20,12},{12,4},{4,0},{1,9},{9... | collective-permute-start | bytes 1572872 | tf_op jit(solution)/shard_map/ppermute | solution.py:56
  681.3 30.7 %collective-permute-start.53 = (bf16[128,2048]{1,0:T(8,128)(2,1)S(1)}, bf16[128,2048]{1,0:T(8,128)(2,1)}, u32[]{:S(2)}, u32[]{:S(2)}) collective-permute-start(bf16[128,2048]{1,0:T(8,128)(2,1)S(1)} %pad_maximum_fusion.14), channel_id=1, source_target_pairs={{8,0},{16,8},{24,16},{28,24},{20,28},{12,20},{4,12},{0,4},{9,1},{1... | collective-permute-start | bytes 1572872 | tf_op jit(solution)/shard_map/ppermute | solution.py:87
  689.4 16.4 %collective-permute-start.62 = (bf16[64,2048]{1,0:T(8,128)(2,1)S(1)}, bf16[64,2048]{1,0:T(8,128)(2,1)S(1)}, u32[]{:S(2)}, u32[]{:S(2)}) collective-permute-start(bf16[64,2048]{1,0:T(8,128)(2,1)S(1)} %slice.453), channel_id=1, source_target_pairs={{0,8},{8,16},{16,24},{24,28},{28,20},{20,12},{12,4},{4,0},{1,9},{9... | collective-permute-start | bytes 786440 | tf_op jit(solution)/shard_map/ppermute | solution.py:60
  733.4 24.5 %collective-permute-start.30 = (bf16[128,2048]{1,0:T(8,128)(2,1)}, bf16[128,2048]{1,0:T(8,128)(2,1)}, u32[]{:S(2)}, u32[]{:S(2)}) collective-permute-start(bf16[128,2048]{1,0:T(8,128)(2,1)} %get-tuple-element.113), channel_id=1, source_target_pairs={{8,0},{16,8},{24,16},{28,24},{20,28},{12,20},{4,12},{0,4},{9,1},{1... | collective-permute-start | bytes 1572872 | tf_op jit(solution)/shard_map/ppermute | solution.py:87
  745.8 16.4 %collective-permute-start.27 = (bf16[128,2048]{1,0:T(8,128)(2,1)}, bf16[128,2048]{1,0:T(8,128)(2,1)}, u32[]{:S(2)}, u32[]{:S(2)}) collective-permute-start(bf16[128,2048]{1,0:T(8,128)(2,1)} %get-tuple-element.112), channel_id=1, source_target_pairs={{0,8},{8,16},{16,24},{24,28},{28,20},{20,12},{12,4},{4,0},{1,9},{9... | collective-permute-start | bytes 1572872 | tf_op jit(solution)/shard_map/ppermute | solution.py:86
  754.4 36.8 %all-to-all-start.3 = ((bf16[8,64,768]{2,1,0:T(8,128)(2,1)}), bf16[8,64,768]{2,1,0:T(8,128)(2,1)S(1)}, u32[]{:S(2)}, u32[]{:S(2)}) async-start(bf16[8,64,768]{2,1,0:T(8,128)(2,1)} %reduce-scatter.6.cloned.1.call-done), calls=%async_computation.4 | async-start | bytes 1572864 | tf_op jit(solution)/shard_map/all_to_all | solution.py:299
  759.3 26.1 %collective-permute-start.31 = (bf16[128,2048]{1,0:T(8,128)(2,1)S(1)}, bf16[128,2048]{1,0:T(8,128)(2,1)S(1)}, u32[]{:S(2)}, u32[]{:S(2)}) collective-permute-start(bf16[128,2048]{1,0:T(8,128)(2,1)S(1)} %fusion.60), channel_id=1, source_target_pairs={{8,0},{16,8},{24,16},{28,24},{20,28},{12,20},{4,12},{0,4},{9,1},{1... | collective-permute-start | bytes 1572872 | tf_op jit(solution)/shard_map/ppermute | solution.py:87
  (125 other events, 1752.4 us)
Sparse Core Ops, SparseCore 0:
  37.6 28.0 all-gather.6
  68.6 92.0 all-gather.8
  162.2 65.0 all-gather.10
  228.8 58.2 all-gather.12
  288.5 58.2 all-gather.14
  570.5 33.8 reduce-scatter.5
  607.1 71.6 reduce-scatter.13
  681.4 73.4 reduce-scatter.11
  757.6 71.7 reduce-scatter.9
  832.4 31.4 reduce-scatter.7
where the time goes:
time: 878 us; the launch traced here: 871 us
  waiting for transfers between devices  278 us (32%)
  matrix products  220 us (25%)
  blocking collectives  121 us (14%)
  other arithmetic  99 us (11%)
  starting transfers between devices  79 us (9%)
  local copies, waits for them, and re-layouts  56.9 us (6%)
  between operations  17.3 us (2%)
    dot_general x37, matrix products, dot(): return lax.dot_general(a, b, (dims, ((), ())), preferred_element_type=F32)  218 us
    ppermute x15, waiting for transfers between devices, gather_ring(): l = lax.ppermute(l, 'head', left)  58.9 us
    all_gather x1, blocking collectives, body(): small = lax.all_gather(small, both, axis=0, tiled=True)  53.5 us
    ppermute x15, waiting for transfers between devices, gather_ring(): r = lax.ppermute(r, 'head', right)  49.1 us
    ppermute x9, waiting for transfers between devices, scatter_ring(): r = lax.ppermute(br.astype(BF), 'head', right)  34.1 us
    ppermute x9, waiting for transfers between devices, scatter_ring(): l = lax.ppermute(bl.astype(BF), 'head', left)  32.8 us
    reduce_scatter x1, waiting for transfers between devices, body(): lax.psum_scatter(grad_out_w, 'fsdp', scatter_dimension=0, tiled=True)  30.4 us
    all_to_all x1, blocking collectives, body(): cols = lax.all_to_all(cols, 'head', split_axis=0, concat_axis=0, tiled=True)  27.5 us
  transfers between devices with their start and end apart: 78, of which 43 were waited for; matrix products, arithmetic and copies ran while one was open for 29% of the time, Pallas kernels for 0%

commit v1 on v0

--- a/solution.py
+++ b/solution.py
@@ -14,6 +14,18 @@
 NEGATIVE = -1e30
 BF = jnp.bfloat16
 F32 = jnp.float32
+
+
+def compute_limits_here(s0, axis_k, v0):
+    finding = s0.shape
+    work_now = s0.reshape(*finding[:axis_k], v0, finding[axis_k] // v0, *finding[axis_k + 1 :])
+    return jnp.moveaxis(work_now, axis_k, 0)
+
+
+def things_search(q_in, where_dim):
+    v_next = list(q_in.shape[1:])
+    v_next[where_dim] *= q_in.shape[0]
+    return jnp.moveaxis(q_in, 0, where_dim).reshape(v_next)
 
 
 def ring_head(n, k):
@@ -146,7 +158,24 @@
     gains_q = lax.dynamic_slice_in_dim(small[:, experts + 2], me * dh, dh, 0).astype(F32)
     gains_k = lax.dynamic_slice_in_dim(small[:, experts + 3], me * dh, dh, 0).astype(F32)
     cols = w_qkv.reshape(shard, 3, n, dh).transpose(2, 0, 1, 3).reshape(n, shard, 3 * dh)
-    cols = lax.all_to_all(cols, "head", split_axis=0, concat_axis=0, tiled=True)
+
+    def trees_show(my_tile, axis_id, shard_in, u_in):
+        u1, a_now = (lax.psum(1, axis_id), lax.axis_index(axis_id))
+        oldest = compute_limits_here(my_tile, shard_in, u1)
+        steps_seen = [oldest[a_now]]
+        for tick in range(1, u1):
+            current_value = oldest[a_now ^ tick]
+            steps_seen.append(
+                lax.ppermute(
+                    current_value,
+                    axis_name=axis_id,
+                    perm=[(dev_j, dev_j ^ tick) for dev_j in range(u1)],
+                )
+            )
+        oldest = jnp.stack(steps_seen)[a_now ^ jnp.arange(u1)]
+        return things_search(oldest, u_in)
+
+    cols = trees_show(cols, "head", 0, 0)
     qkv = lax.all_gather(cols, "fsdp", axis=1, tiled=True).reshape(width, 3 * dh)
     tokens_all = gather_ring(hidden[0]).reshape(seq, width)
     info = gather_ring(jnp.concatenate([routes[0], route_codes[0]], axis=1)).reshape(seq, 2 * TOP)

time: 878 us -> 879 us (level)
  blocking collectives: 121 us -> 95.6 us
  starting transfers between devices: 79 us -> 92.7 us
  waiting for transfers between devices: 278 us -> 288 us
    all_to_all x1 -> x0, blocking collectives: 27.5 us -> none  [body(): cols = lax.all_to_all(cols, 'head', split_axis=0, concat_axis=0, tiled=True)]
    ppermute x0 -> x7, starting transfers between devices: none -> 12.6 us  [trees_show(): lax.ppermute(current_value, axis_name=axis_id, perm=[(dev_j, dev_j ^ tick...]
    ppermute x0 -> x7, waiting for transfers between devices: none -> 10.1 us  [trees_show(): lax.ppermute(current_value, axis_name=axis_id, perm=[(dev_j, dev_j ^ tick...]
    unnamed x195 -> x201, local copies, waits for them, and re-layouts: 18.9 us -> 18.9 us
  transfers between devices with their start and end apart: 78 -> 85, of which waited for: 43 -> 45; matrix products, arithmetic and copies ran while one was open for 29% -> 29% of each run, Pallas kernels for 0% -> 0%
where the time goes in v1:
time: 879 us; the launch traced here: 871 us
  waiting for transfers between devices  288 us (33%)
  matrix products  220 us (25%)
  other arithmetic  99.4 us (11%)
  blocking collectives  95.6 us (11%)
  starting transfers between devices  92.7 us (11%)
  local copies, waits for them, and re-layouts  58.4 us (7%)
  between operations  17.5 us (2%)
    dot_general x37, matrix products, dot(): return lax.dot_general(a, b, (dims, ((), ())), preferred_element_type=F32)  218 us
    ppermute x15, waiting for transfers between devices, gather_ring(): l = lax.ppermute(l, 'head', left)  58 us
    all_gather x1, blocking collectives, body(): small = lax.all_gather(small, both, axis=0, tiled=True)  54.8 us
    ppermute x15, waiting for transfers between devices, gather_ring(): r = lax.ppermute(r, 'head', right)  45 us
    ppermute x9, waiting for transfers between devices, scatter_ring(): r = lax.ppermute(br.astype(BF), 'head', right)  39.6 us
    ppermute x9, waiting for transfers between devices, scatter_ring(): l = lax.ppermute(bl.astype(BF), 'head', left)  33.4 us
    reduce_scatter x1, waiting for transfers between devices, body(): lax.psum_scatter(grad_out_w, 'fsdp', scatter_dimension=0, tiled=True)  30.3 us
    reduce_scatter x3, waiting for transfers between devices, over_fsdp(): lax.psum_scatter(jnp.stack(grads), 'fsdp', scatter_dimension=1, tiled=True)  26.6 us
  transfers between devices with their start and end apart: 85, of which 45 were waited for; matrix products, arithmetic and copies ran while one was open for 29% of the time, Pallas kernels for 0%

profile of v1, /device:TPU:0, one launch (start us, length us, event | category | flops | bytes accessed | tf_op | source)
XLA Modules:
  0.0 871.4 jit_solution(6315554258676717538)
XLA Ops:
  22.8 10.1 %collective-permute-done.12 = bf16[1,64,768]{2,1,0:T(8,128)(2,1)S(1)} collective-permute-done((bf16[1,64,768]{2,1,0:T(8,128)(2,1)S(1)}, bf16[1,64,768]{2,1,0:T(8,128)(2,1)S(1)}, u32[]{:S(2)}, u32[]{:S(2)}) %collective-permute-start.12) | collective-permute-done | bytes 98336 | tf_op jit(solution)/shard_map/ppermute | solution.py:169
  44.9 54.8 %all-gather.1 = bf16[32,64,20]{1,2,0:T(8,128)(2,1)S(1)} all-gather(bf16[1,64,20]{1,2,0:T(8,128)(2,1)S(1)} %bitcast.528), channel_id=1, replica_groups=mesh['head'=8,'fsdp'=4] {'head','fsdp'}, dimensions={0}, use_global_device_ids=true | all-gather | bytes 84480 | tf_op jit(solution)/shard_map/all_gather | solution.py:154
  128.0 24.9 %collective-permute-done.40 = bf16[128,2048]{1,0:T(8,128)(2,1)} collective-permute-done((bf16[128,2048]{1,0:T(8,128)(2,1)S(1)}, bf16[128,2048]{1,0:T(8,128)(2,1)}, u32[]{:S(2)}, u32[]{:S(2)}) %collective-permute-start.40) | collective-permute-done | bytes 524320 | tf_op jit(solution)/shard_map/ppermute | solution.py:69
  157.6 6.7 collective-permute-done.3
  167.1 8.4 collective-permute-done.42
  179.3 7.4 collective-permute-done.5
  190.4 7.6 collective-permute-done.44
  213.4 7.9 fusion.133
  221.5 21.0 %psum.14 = f32[2,1024]{1,0:T(2,128)} all-reduce(f32[2,1024]{1,0:T(2,128)S(1)} %pad_maximum_fusion.17), channel_id=1, replica_groups=mesh['head'=8,'fsdp'=4] {'head'}, use_global_device_ids=true, to_apply=%region_3.4 | all-reduce | flops 2048 | bytes 16384 | tf_op jit(solution)/shard_map/psum | solution.py:199
  259.1 8.8 %collective-permute-done.15 = bf16[1024,256]{0,1:T(8,128)(2,1)S(1)} collective-permute-done((bf16[1024,256]{0,1:T(8,128)(2,1)S(1)}, bf16[1024,256]{0,1:T(8,128)(2,1)S(1)}, u32[]{:S(2)}, u32[]{:S(2)}) %collective-permute-start.15) | collective-permute-done | bytes 524320 | tf_op jit(solution)/shard_map/ppermute | solution.py:68
  286.4 6.9 collective-permute-done.19
  300.7 14.3 %multiply_reduce_fusion = (f32[1024]{0:T(1024)S(1)}, f32[1024,2048]{1,0:T(8,128)S(1)}) fusion(bf16[1024,2048]{0,1:T(8,128)(2,1)} %bitcast.54, bf16[2048,2048]{1,0:T(8,128)(2,1)} %all-gather.8.cloned.1.call-done, bf16[8,128,2048]{2,1,0:T(8,128)(2,1)} %fusion.75), kind=kOutput, calls=%fused_computation.31 | convolution fusion | flops 8598322176 | bytes 25169920 | tf_op jit(solution)/shard_map/dot_general | solution.py:115
  322.0 5.7 fusion.4
  327.6 10.1 %fusion.18 = f32[1024,1024]{1,0:T(8,128)} fusion(bf16[1024,2048]{1,0:T(8,128)(2,1)} %copy-done.6, bf16[2,2048,1024]{2,1,0:T(8,128)(2,1)} %all-gather.10.cloned.1.call-done), kind=kOutput, calls=%fused_computation.68 | convolution fusion | flops 4294967296 | bytes 12582912 | tf_op jit(solution)/shard_map/dot_general | solution.py:115
  337.7 6.4 fusion.23
  344.2 10.1 %fusion.20 = f32[1024,1024]{1,0:T(8,128)} fusion(bf16[1024,2048]{1,0:T(8,128)(2,1)} %copy-done.6, bf16[2,2048,1024]{2,1,0:T(8,128)(2,1)} %all-gather.12.cloned.1.call-done), kind=kOutput, calls=%fused_computation.70 | convolution fusion | flops 4294967296 | bytes 12582912 | tf_op jit(solution)/shard_map/dot_general | solution.py:115
  354.4 6.1 fusion.24
  360.5 12.2 %multiply_convert_fusion.5 = (bf16[1024,1024]{1,0:T(8,128)(2,1)S(1)}, bf16[1024,1024]{1,0:T(8,128)(2,1)S(1)}, bf16[1024,1024]{1,0:T(8,128)(2,1)}) fusion(f32[1024,1024]{1,0:T(8,128)} %fusion.18, f32[1024,1024]{1,0:T(8,128)} %fusion.20, bf16[1024,2048]{1,0:T(8,128)(2,1)} %bitcast.485, bf16[2,1024,2048]{2,1,0:T(8,128)(2,1)} %all-gather.14.cloned.1.call-done), kind=kOutput, calls=%fused_computation.50 | convolution fusion | flops 4310695936 | bytes 23068672 | tf_op jit(solution)/shard_map/dot_general | solution.py:115
  372.7 10.4 %fusion.17 = f32[1024,2048]{1,0:T(8,128)} fusion(bf16[1024,1024]{1,0:T(8,128)(2,1)S(1)} %get-tuple-element.89, bf16[2,2048,1024]{2,1,0:T(8,128)(2,1)} %all-gather.10.cloned.1.call-done), kind=kOutput, calls=%fused_computation.67 | convolution fusion | flops 4294967296 | bytes 14680064 | tf_op jit(solution)/shard_map/dot_general | solution.py:115
  383.1 9.1 %fusion.19 = f32[1024,2048]{1,0:T(8,128)} fusion(bf16[1024,1024]{1,0:T(8,128)(2,1)S(1)} %get-tuple-element.88, bf16[2,2048,1024]{2,1,0:T(8,128)(2,1)} %all-gather.12.cloned.1.call-done), kind=kOutput, calls=%fused_computation.69 | convolution fusion | flops 4294967296 | bytes 14680064 | tf_op jit(solution)/shard_map/dot_general | solution.py:115
  392.3 10.4 %multiply_convert_fusion.3 = (bf16[1024,1024]{1,0:T(8,128)(2,1)S(1)}, bf16[1024,1024]{1,0:T(8,128)(2,1)}, bf16[1024,1024]{1,0:T(8,128)(2,1)}) fusion(f32[1024,1024]{1,0:T(8,128)} %fusion.23, f32[1024,1024]{1,0:T(8,128)} %fusion.24, bf16[1024,2048]{1,0:T(8,128)(2,1)S(1)} %bitcast.484, bf16[2,1024,2048]{2,1,0:T(8,128)(2,1)S(1)} %bitcast.562), kind=kOutput, calls=%fused_computation.48 | convolution fusion | flops 4310695936 | bytes 23068672 | tf_op jit(solution)/shard_map/dot_general | solution.py:115
  402.7 9.1 %fusion.22 = f32[1024,2048]{1,0:T(8,128)} fusion(bf16[1024,1024]{1,0:T(8,128)(2,1)} %get-tuple-element.86, bf16[2,2048,1024]{2,1,0:T(8,128)(2,1)S(1)} %bitcast.564), kind=kOutput, calls=%fused_computation.72 | convolution fusion | flops 4294967296 | bytes 14680064 | tf_op jit(solution)/shard_map/dot_general | solution.py:115
  411.9 13.3 %add_convert_fusion = bf16[1024,2048]{1,0:T(8,128)(2,1)} fusion(f32[1024,2048]{1,0:T(8,128)} %fusion.22, f32[1024,2048]{1,0:T(8,128)} %fusion.17, f32[1024,2048]{1,0:T(8,128)} %fusion.19, bf16[1024,1024]{1,0:T(8,128)(2,1)S(1)} %get-tuple-element.85, bf16[2,2048,1024]{2,1,0:T(8,128)(2,1)} %all-gather.12.cloned.1.call-done), kind=kOutput, calls=%fused_computation.29 | convolution fusion | flops 4303355904 | bytes 35651584 | tf_op jit(solution)/shard_map/dot_general | solution.py:115
  428.9 7.2 collective-permute-done.47
  439.6 12.6 %collective-permute-done.48 = bf16[128,2048]{1,0:T(8,128)(2,1)S(1)} collective-permute-done((bf16[128,2048]{1,0:T(8,128)(2,1)S(1)}, bf16[128,2048]{1,0:T(8,128)(2,1)S(1)}, u32[]{:S(2)}, u32[]{:S(2)}) %collective-permute-start.48) | collective-permute-done | bytes 524320 | tf_op jit(solution)/shard_map/ppermute | solution.py:98
  453.7 7.5 convolution_convert_fusion.1
  466.0 12.6 %fusion.2 = (f32[1024]{0:T(1024)S(1)}, f32[1024]{0:T(1024)S(1)}, bf16[1024,2048]{1,0:T(8,128)(2,1)}, bf16[1024,2048]{1,0:T(8,128)(2,1)}, bf16[1024,2048]{1,0:T(8,128)(2,1)}) fusion(bf16[8,128,2048]{2,1,0:T(8,128)(2,1)} %fusion.77, bf16[1024,2048]{1,0:T(8,128)(2,1)S(1)} %convolution_convert_fusion.1, f32[1024]{0:T(1024)S(1)} %bitcast.532, ...), kind=kOutput, calls=%fused_computation.7 | convolution fusion | flops 4328519680 | bytes 27279360 | tf_op jit(solution)/shard_map/dot_general | solution.py:115
  502.7 6.5 convolution_convert_fusion.4
  543.0 19.8 %psum.15 = f32[2,1024]{1,0:T(2,128)S(1)} all-reduce(f32[2,1024]{1,0:T(2,128)S(1)} %pad_maximum_fusion.18), channel_id=1, replica_groups=mesh['head'=8,'fsdp'=4] {'head'}, use_global_device_ids=true, to_apply=%region_23.24 | all-reduce | flops 2048 | bytes 16384 | tf_op jit(solution)/shard_map/psum | solution.py:313
  570.8 7.7 convert_bitcast_fusion.1
  578.5 6.2 convert_bitcast_fusion
  584.8 6.3 pad_maximum_fusion.2
  591.1 7.6 convert_bitcast_fusion.3
  598.8 6.3 convert_bitcast_fusion.2
  605.1 6.3 pad_maximum_fusion.1
  613.2 7.5 convert_bitcast_fusion.5
  620.8 6.2 convert_bitcast_fusion.4
  627.0 6.3 pad_maximum_fusion
  647.6 7.8 collective-permute-done.63
  657.6 5.7 convolution_convert_fusion
  663.7 11.4 %collective-permute-done.65 = bf16[128,2048]{1,0:T(8,128)(2,1)S(1)} collective-permute-done((bf16[128,2048]{1,0:T(8,128)(2,1)S(1)}, bf16[128,2048]{1,0:T(8,128)(2,1)S(1)}, u32[]{:S(2)}, u32[]{:S(2)}) %collective-permute-start.65) | collective-permute-done | bytes 524320 | tf_op jit(solution)/shard_map/ppermute | solution.py:68
  690.0 8.3 collective-permute-done.56
  698.4 5.5 collective-permute-done.69
  707.8 10.3 %collective-permute-done.57 = bf16[128,2048]{1,0:T(8,128)(2,1)} collective-permute-done((bf16[128,2048]{1,0:T(8,128)(2,1)S(1)}, bf16[128,2048]{1,0:T(8,128)(2,1)}, u32[]{:S(2)}, u32[]{:S(2)}) %collective-permute-start.57) | collective-permute-done | bytes 524320 | tf_op jit(solution)/shard_map/ppermute | solution.py:98
  747.8 6.9 all-to-all-done.3
  762.1 23.5 %collective-permute-done.38 = bf16[128,2048]{1,0:T(8,128)(2,1)S(1)} collective-permute-done((bf16[128,2048]{1,0:T(8,128)(2,1)S(1)}, bf16[128,2048]{1,0:T(8,128)(2,1)S(1)}, u32[]{:S(2)}, u32[]{:S(2)}) %collective-permute-start.38) | collective-permute-done | bytes 524320 | tf_op jit(solution)/shard_map/ppermute | solution.py:99
  803.1 26.6 %reduce-scatter.10.cloned.1.call-done = bf16[2,512,1024]{2,1,0:T(8,128)(2,1)} async-done(((bf16[2,2048,1024]{2,1,0:T(8,128)(2,1)}), bf16[2,512,1024]{2,1,0:T(8,128)(2,1)}) %reduce-scatter.10.cloned.1.call-update) | async-done | bytes 2097168 | tf_op jit(solution)/shard_map/reduce_scatter | solution.py:263
  833.8 30.3 %reduce-scatter.8.cloned.1.call-done = f32[64,2048]{1,0:T(8,128)} async-done(((f32[256,2048]{1,0:T(8,128)}), f32[64,2048]{1,0:T(8,128)}) %reduce-scatter.8.cloned.1.call-update) | async-done | bytes 524304 | tf_op jit(solution)/shard_map/reduce_scatter | solution.py:332
  (535 shorter events, 309.4 us)
Async XLA Ops:
  7.2 206.3 %all-gather.16.cloned.1.call-start = ((), (), s32[]{:S(2)}) async-start(), calls=%async_computation.18 | async-start | bytes 3932160 | tf_op jit(solution)/shard_map/all_gather | solution.py:179
  17.7 15.2 %collective-permute-start.12 = (bf16[1,64,768]{2,1,0:T(8,128)(2,1)S(1)}, bf16[1,64,768]{2,1,0:T(8,128)(2,1)S(1)}, u32[]{:S(2)}, u32[]{:S(2)}) collective-permute-start(bf16[1,64,768]{2,1,0:T(8,128)(2,1)S(1)} %get-tuple-element.134), channel_id=1, source_target_pairs={{0,20},{4,16},{8,28},{12,24},{16,4},{20,0},{24,12},{28,8},{1,21},{... | collective-permute-start | bytes 294920 | tf_op jit(solution)/shard_map/ppermute | solution.py:169
  34.5 266.2 %all-gather.8.cloned.1.call-start = ((), (), s32[]{:S(2)}) async-start(), calls=%async_computation.9 | async-start | bytes 8650752 | tf_op jit(solution)/shard_map/all_gather | solution.py:182
  35.3 292.4 %all-gather.10.cloned.1.call-start = ((), (), s32[]{:S(2)}) async-start(), calls=%async_computation.10 | async-start | bytes 10485760 | tf_op jit(solution)/shard_map/all_gather | solution.py:183
  36.0 308.2 %all-gather.12.cloned.1.call-start = ((), (), s32[]{:S(2)}) async-start(), calls=%async_computation.11 | async-start | bytes 10485760 | tf_op jit(solution)/shard_map/all_gather | solution.py:184
  36.6 323.9 %all-gather.14.cloned.1.call-start = ((), (), s32[]{:S(2)}) async-start(), calls=%async_computation.12 | async-start | bytes 10485760 | tf_op jit(solution)/shard_map/all_gather | solution.py:185
  36.6 73.1 %collective-permute-start.23 = (s32[128,16]{0,1:T(8,128)S(1)}, s32[128,16]{0,1:T(8,128)S(1)}, u32[]{:S(2)}, u32[]{:S(2)}) collective-permute-start(s32[128,16]{0,1:T(8,128)S(1)} %pad_add_fusion), channel_id=1, source_target_pairs={{0,8},{8,16},{16,24},{24,28},{28,20},{20,12},{12,4},{4,0},{1,9},{9... | collective-permute-start | bytes 24584 | tf_op jit(solution)/shard_map/ppermute | solution.py:68
  40.6 69.2 %collective-permute-start.24 = (s32[128,16]{0,1:T(8,128)S(1)}, s32[128,16]{0,1:T(8,128)S(1)}, u32[]{:S(2)}, u32[]{:S(2)}) collective-permute-start(s32[128,16]{0,1:T(8,128)S(1)} %pad_add_fusion), channel_id=1, source_target_pairs={{8,0},{16,8},{24,16},{28,24},{20,28},{12,20},{4,12},{0,4},{9,1},{1... | collective-permute-start | bytes 24584 | tf_op jit(solution)/shard_map/ppermute | solution.py:69
  40.6 82.6 %collective-permute-start = (bf16[128,2048]{1,0:T(8,128)(2,1)S(1)}, bf16[128,2048]{1,0:T(8,128)(2,1)S(1)}, u32[]{:S(2)}, u32[]{:S(2)}) collective-permute-start(bf16[128,2048]{1,0:T(8,128)(2,1)S(1)} %bitcast.451), channel_id=1, source_target_pairs={{0,8},{8,16},{16,24},{24,28},{28,20},{20,12},{12,4},{4,0},{1,9},{9... | collective-permute-start | bytes 1572872 | tf_op jit(solution)/shard_map/ppermute | solution.py:68
  42.7 81.6 %collective-permute-start.1 = (bf16[128,2048]{1,0:T(8,128)(2,1)S(1)}, bf16[128,2048]{1,0:T(8,128)(2,1)S(1)}, u32[]{:S(2)}, u32[]{:S(2)}) collective-permute-start(bf16[128,2048]{1,0:T(8,128)(2,1)S(1)} %bitcast.452), channel_id=1, source_target_pairs={{8,0},{16,8},{24,16},{28,24},{20,28},{12,20},{4,12},{0,4},{9,1},{1... | collective-permute-start | bytes 1572872 | tf_op jit(solution)/shard_map/ppermute | solution.py:69
  42.7 84.3 %collective-permute-start.39 = (bf16[128,2048]{1,0:T(8,128)(2,1)S(1)}, bf16[128,2048]{1,0:T(8,128)(2,1)S(1)}, u32[]{:S(2)}, u32[]{:S(2)}) collective-permute-start(bf16[128,2048]{1,0:T(8,128)(2,1)S(1)} %bitcast.465), channel_id=1, source_target_pairs={{0,8},{8,16},{16,24},{24,28},{28,20},{20,12},{12,4},{4,0},{1,9},{9... | collective-permute-start | bytes 1572872 | tf_op jit(solution)/shard_map/ppermute | solution.py:68
  121.2 31.6 %collective-permute-start.40 = (bf16[128,2048]{1,0:T(8,128)(2,1)S(1)}, bf16[128,2048]{1,0:T(8,128)(2,1)}, u32[]{:S(2)}, u32[]{:S(2)}) collective-permute-start(bf16[128,2048]{1,0:T(8,128)(2,1)S(1)} %bitcast.466), channel_id=1, source_target_pairs={{8,0},{16,8},{24,16},{28,24},{20,28},{12,20},{4,12},{0,4},{9,1},{1... | collective-permute-start | bytes 1572872 | tf_op jit(solution)/shard_map/ppermute | solution.py:69
  123.3 31.5 %collective-permute-start.2 = (bf16[128,2048]{1,0:T(8,128)(2,1)S(1)}, bf16[128,2048]{1,0:T(8,128)(2,1)S(1)}, u32[]{:S(2)}, u32[]{:S(2)}) collective-permute-start(bf16[128,2048]{1,0:T(8,128)(2,1)S(1)} %collective-permute-done), channel_id=1, source_target_pairs={{0,8},{8,16},{16,24},{24,28},{28,20},{20,12},{12,4},{4,0},{1,9},{9... | collective-permute-start | bytes 1572872 | tf_op jit(solution)/shard_map/ppermute | solution.py:68
  124.3 40.0 %collective-permute-start.3 = (bf16[128,2048]{1,0:T(8,128)(2,1)S(1)}, bf16[128,2048]{1,0:T(8,128)(2,1)S(1)}, u32[]{:S(2)}, u32[]{:S(2)}) collective-permute-start(bf16[128,2048]{1,0:T(8,128)(2,1)S(1)} %collective-permute-done.1), channel_id=1, source_target_pairs={{8,0},{16,8},{24,16},{28,24},{20,28},{12,20},{4,12},{0,4},{9,1},{1... | collective-permute-start | bytes 1572872 | tf_op jit(solution)/shard_map/ppermute | solution.py:69
  127.0 37.3 %collective-permute-start.41 = (bf16[128,2048]{1,0:T(8,128)(2,1)S(1)}, bf16[128,2048]{1,0:T(8,128)(2,1)S(1)}, u32[]{:S(2)}, u32[]{:S(2)}) collective-permute-start(bf16[128,2048]{1,0:T(8,128)(2,1)S(1)} %collective-permute-done.39), channel_id=1, source_target_pairs={{0,8},{8,16},{16,24},{24,28},{28,20},{20,12},{12,4},{4,0},{1,9},{9... | collective-permute-start | bytes 1572872 | tf_op jit(solution)/shard_map/ppermute | solution.py:68
  152.8 22.7 %collective-permute-start.42 = (bf16[128,2048]{1,0:T(8,128)(2,1)}, bf16[128,2048]{1,0:T(8,128)(2,1)S(1)}, u32[]{:S(2)}, u32[]{:S(2)}) collective-permute-start(bf16[128,2048]{1,0:T(8,128)(2,1)} %collective-permute-done.40), channel_id=1, source_target_pairs={{8,0},{16,8},{24,16},{28,24},{20,28},{12,20},{4,12},{0,4},{9,1},{1... | collective-permute-start | bytes 1572872 | tf_op jit(solution)/shard_map/ppermute | solution.py:69
  154.8 22.5 %collective-permute-start.4 = (bf16[128,2048]{1,0:T(8,128)(2,1)S(1)}, bf16[128,2048]{1,0:T(8,128)(2,1)S(1)}, u32[]{:S(2)}, u32[]{:S(2)}) collective-permute-start(bf16[128,2048]{1,0:T(8,128)(2,1)S(1)} %collective-permute-done.2), channel_id=1, source_target_pairs={{0,8},{8,16},{16,24},{24,28},{28,20},{20,12},{12,4},{4,0},{1,9},{9... | collective-permute-start | bytes 1572872 | tf_op jit(solution)/shard_map/ppermute | solution.py:68
  164.3 22.5 %collective-permute-start.5 = (bf16[128,2048]{1,0:T(8,128)(2,1)S(1)}, bf16[128,2048]{1,0:T(8,128)(2,1)S(1)}, u32[]{:S(2)}, u32[]{:S(2)}) collective-permute-start(bf16[128,2048]{1,0:T(8,128)(2,1)S(1)} %collective-permute-done.3), channel_id=1, source_target_pairs={{8,0},{16,8},{24,16},{28,24},{20,28},{12,20},{4,12},{0,4},{9,1},{1... | collective-permute-start | bytes 1572872 | tf_op jit(solution)/shard_map/ppermute | solution.py:69
  164.3 22.6 %collective-permute-start.43 = (bf16[128,2048]{1,0:T(8,128)(2,1)S(1)}, bf16[128,2048]{1,0:T(8,128)(2,1)S(1)}, u32[]{:S(2)}, u32[]{:S(2)}) collective-permute-start(bf16[128,2048]{1,0:T(8,128)(2,1)S(1)} %collective-permute-done.41), channel_id=1, source_target_pairs={{0,8},{8,16},{16,24},{24,28},{28,20},{20,12},{12,4},{4,0},{1,9},{9... | collective-permute-start | bytes 1572872 | tf_op jit(solution)/shard_map/ppermute | solution.py:68
  175.5 22.5 %collective-permute-start.44 = (bf16[128,2048]{1,0:T(8,128)(2,1)S(1)}, bf16[128,2048]{1,0:T(8,128)(2,1)S(1)}, u32[]{:S(2)}, u32[]{:S(2)}) collective-permute-start(bf16[128,2048]{1,0:T(8,128)(2,1)S(1)} %collective-permute-done.42), channel_id=1, source_target_pairs={{8,0},{16,8},{24,16},{28,24},{20,28},{12,20},{4,12},{0,4},{9,1},{1... | collective-permute-start | bytes 1572872 | tf_op jit(solution)/shard_map/ppermute | solution.py:69
  177.3 24.3 %collective-permute-start.6 = (bf16[64,2048]{1,0:T(8,128)(2,1)S(1)}, bf16[64,2048]{1,0:T(8,128)(2,1)S(1)}, u32[]{:S(2)}, u32[]{:S(2)}) collective-permute-start(bf16[64,2048]{1,0:T(8,128)(2,1)S(1)} %slice.412), channel_id=1, source_target_pairs={{0,8},{8,16},{16,24},{24,28},{28,20},{20,12},{12,4},{4,0},{1,9},{9... | collective-permute-start | bytes 786440 | tf_op jit(solution)/shard_map/ppermute | solution.py:72
  186.8 16.8 %collective-permute-start.7 = (bf16[64,2048]{1,0:T(8,128)(2,1)S(1)}, bf16[64,2048]{1,0:T(8,128)(2,1)S(1)}, u32[]{:S(2)}, u32[]{:S(2)}) collective-permute-start(bf16[64,2048]{1,0:T(8,128)(2,1)S(1)} %slice.413), channel_id=1, source_target_pairs={{8,0},{16,8},{24,16},{28,24},{20,28},{12,20},{4,12},{0,4},{9,1},{1... | collective-permute-start | bytes 786440 | tf_op jit(solution)/shard_map/ppermute | solution.py:73
  188.4 81.9 %collective-permute-start.45 = (bf16[64,2048]{1,0:T(8,128)(2,1)}, bf16[64,2048]{1,0:T(8,128)(2,1)}, u32[]{:S(2)}, u32[]{:S(2)}) collective-permute-start(bf16[64,2048]{1,0:T(8,128)(2,1)} %slice.445), channel_id=1, source_target_pairs={{0,8},{8,16},{16,24},{24,28},{28,20},{20,12},{12,4},{4,0},{1,9},{9... | collective-permute-start | bytes 786440 | tf_op jit(solution)/shard_map/ppermute | solution.py:72
  199.5 70.8 %collective-permute-start.46 = (bf16[64,2048]{1,0:T(8,128)(2,1)}, bf16[64,2048]{1,0:T(8,128)(2,1)}, u32[]{:S(2)}, u32[]{:S(2)}) collective-permute-start(bf16[64,2048]{1,0:T(8,128)(2,1)} %slice.446), channel_id=1, source_target_pairs={{8,0},{16,8},{24,16},{28,24},{20,28},{12,20},{4,12},{0,4},{9,1},{1... | collective-permute-start | bytes 786440 | tf_op jit(solution)/shard_map/ppermute | solution.py:73
  437.4 14.8 %collective-permute-start.48 = (bf16[128,2048]{1,0:T(8,128)(2,1)S(1)}, bf16[128,2048]{1,0:T(8,128)(2,1)S(1)}, u32[]{:S(2)}, u32[]{:S(2)}) collective-permute-start(bf16[128,2048]{1,0:T(8,128)(2,1)S(1)} %pad_maximum_fusion.11), channel_id=1, source_target_pairs={{0,8},{8,16},{16,24},{24,28},{28,20},{20,12},{12,4},{4,0},{1,9},{9... | collective-permute-start | bytes 1572872 | tf_op jit(solution)/shard_map/ppermute | solution.py:98
  438.3 22.8 %collective-permute-start.52 = (bf16[128,2048]{1,0:T(8,128)(2,1)S(1)}, bf16[128,2048]{1,0:T(8,128)(2,1)S(1)}, u32[]{:S(2)}, u32[]{:S(2)}) collective-permute-start(bf16[128,2048]{1,0:T(8,128)(2,1)S(1)} %pad_maximum_fusion.12), channel_id=1, source_target_pairs={{8,0},{16,8},{24,16},{28,24},{20,28},{12,20},{4,12},{0,4},{9,1},{1... | collective-permute-start | bytes 1572872 | tf_op jit(solution)/shard_map/ppermute | solution.py:99
  464.2 21.7 %collective-permute-start.53 = (bf16[128,2048]{1,0:T(8,128)(2,1)S(1)}, bf16[128,2048]{1,0:T(8,128)(2,1)S(1)}, u32[]{:S(2)}, u32[]{:S(2)}) collective-permute-start(bf16[128,2048]{1,0:T(8,128)(2,1)S(1)} %get-tuple-element.103), channel_id=1, source_target_pairs={{8,0},{16,8},{24,16},{28,24},{20,28},{12,20},{4,12},{0,4},{9,1},{1... | collective-permute-start | bytes 1572872 | tf_op jit(solution)/shard_map/ppermute | solution.py:99
  510.0 14.9 %all-to-all-start.1 = ((bf16[128,8,256]{2,0,1:T(8,128)(2,1)}), bf16[128,8,256]{2,0,1:T(8,128)(2,1)S(1)}, u32[]{:S(2)}, u32[]{:S(2)}) async-start(bf16[128,8,256]{2,0,1:T(8,128)(2,1)} %bitcast.445), calls=%async_computation.1 | async-start | bytes 1048576 | tf_op jit(solution)/shard_map/all_to_all | solution.py:293
  514.6 240.0 %reduce-scatter.6.cloned.1.call-start = ((), (), s32[]{:S(2)}) async-start(), calls=%async_computation.13 | async-start | bytes 3932160 | tf_op jit(solution)/shard_map/reduce_scatter | solution.py:327
  570.6 224.3 %reduce-scatter.14.cloned.1.call-start = ((), (), s32[]{:S(2)}) async-start(), calls=%async_computation.17 | async-start | bytes 10485760 | tf_op jit(solution)/shard_map/reduce_scatter | solution.py:263
  591.1 208.0 %reduce-scatter.12.cloned.1.call-start = ((), (), s32[]{:S(2)}) async-start(), calls=%async_computation.16 | async-start | bytes 10485760 | tf_op jit(solution)/shard_map/reduce_scatter | solution.py:263
  611.4 218.3 %reduce-scatter.10.cloned.1.call-start = ((), (), s32[]{:S(2)}) async-start(), calls=%async_computation.15 | async-start | bytes 10485760 | tf_op jit(solution)/shard_map/reduce_scatter | solution.py:263
  633.4 230.8 %reduce-scatter.8.cloned.1.call-start = ((), (), s32[]{:S(2)}) async-start(), calls=%async_computation.14 | async-start | bytes 2621440 | tf_op jit(solution)/shard_map/reduce_scatter | solution.py:332
  637.2 18.2 %collective-permute-start.63 = (bf16[128,2048]{1,0:T(8,128)(2,1)S(1)}, bf16[128,2048]{1,0:T(8,128)(2,1)S(1)}, u32[]{:S(2)}, u32[]{:S(2)}) collective-permute-start(bf16[128,2048]{1,0:T(8,128)(2,1)S(1)} %copy-done.37), channel_id=1, source_target_pairs={{0,8},{8,16},{16,24},{24,28},{28,20},{20,12},{12,4},{4,0},{1,9},{9... | collective-permute-start | bytes 1572872 | tf_op jit(solution)/shard_map/ppermute | solution.py:68
  637.3 18.1 %collective-permute-start.64 = (bf16[128,2048]{1,0:T(8,128)(2,1)S(1)}, bf16[128,2048]{1,0:T(8,128)(2,1)S(1)}, u32[]{:S(2)}, u32[]{:S(2)}) collective-permute-start(bf16[128,2048]{1,0:T(8,128)(2,1)S(1)} %copy-done.37), channel_id=1, source_target_pairs={{8,0},{16,8},{24,16},{28,24},{20,28},{12,20},{4,12},{0,4},{9,1},{1... | collective-permute-start | bytes 1572872 | tf_op jit(solution)/shard_map/ppermute | solution.py:69
  645.4 85.0 %collective-permute-start.36 = (bf16[128,2048]{1,0:T(8,128)(2,1)S(1)}, bf16[128,2048]{1,0:T(8,128)(2,1)}, u32[]{:S(2)}, u32[]{:S(2)}) collective-permute-start(bf16[128,2048]{1,0:T(8,128)(2,1)S(1)} %pad_maximum_fusion.10), channel_id=1, source_target_pairs={{8,0},{16,8},{24,16},{28,24},{20,28},{12,20},{4,12},{0,4},{9,1},{1... | collective-permute-start | bytes 1572872 | tf_op jit(solution)/shard_map/ppermute | solution.py:99
  646.7 73.4 %collective-permute-start.32 = (bf16[128,2048]{1,0:T(8,128)(2,1)S(1)}, bf16[128,2048]{1,0:T(8,128)(2,1)S(1)}, u32[]{:S(2)}, u32[]{:S(2)}) collective-permute-start(bf16[128,2048]{1,0:T(8,128)(2,1)S(1)} %pad_maximum_fusion.9), channel_id=1, source_target_pairs={{0,8},{8,16},{16,24},{24,28},{28,20},{20,12},{12,4},{4,0},{1,9},{9... | collective-permute-start | bytes 1572872 | tf_op jit(solution)/shard_map/ppermute | solution.py:98
  655.4 19.6 %collective-permute-start.65 = (bf16[128,2048]{1,0:T(8,128)(2,1)S(1)}, bf16[128,2048]{1,0:T(8,128)(2,1)S(1)}, u32[]{:S(2)}, u32[]{:S(2)}) collective-permute-start(bf16[128,2048]{1,0:T(8,128)(2,1)S(1)} %collective-permute-done.63), channel_id=1, source_target_pairs={{0,8},{8,16},{16,24},{24,28},{28,20},{20,12},{12,4},{4,0},{1,9},{9... | collective-permute-start | bytes 1572872 | tf_op jit(solution)/shard_map/ppermute | solution.py:68
  655.4 19.6 %collective-permute-start.66 = (bf16[128,2048]{1,0:T(8,128)(2,1)S(1)}, bf16[128,2048]{1,0:T(8,128)(2,1)S(1)}, u32[]{:S(2)}, u32[]{:S(2)}) collective-permute-start(bf16[128,2048]{1,0:T(8,128)(2,1)S(1)} %collective-permute-done.64), channel_id=1, source_target_pairs={{8,0},{16,8},{24,16},{28,24},{20,28},{12,20},{4,12},{0,4},{9,1},{1... | collective-permute-start | bytes 1572872 | tf_op jit(solution)/shard_map/ppermute | solution.py:69
  663.4 16.7 %collective-permute-start.55 = (bf16[64,2048]{1,0:T(8,128)(2,1)S(1)}, bf16[64,2048]{1,0:T(8,128)(2,1)S(1)}, u32[]{:S(2)}, u32[]{:S(2)}) collective-permute-start(bf16[64,2048]{1,0:T(8,128)(2,1)S(1)} %get-tuple-element.98), channel_id=1, source_target_pairs={{0,8},{8,16},{16,24},{24,28},{28,20},{20,12},{12,4},{4,0},{1,9},{9... | collective-permute-start | bytes 786440 | tf_op jit(solution)/shard_map/ppermute | solution.py:87
  675.1 14.0 %collective-permute-start.67 = (bf16[128,2048]{1,0:T(8,128)(2,1)S(1)}, bf16[128,2048]{1,0:T(8,128)(2,1)S(1)}, u32[]{:S(2)}, u32[]{:S(2)}) collective-permute-start(bf16[128,2048]{1,0:T(8,128)(2,1)S(1)} %collective-permute-done.65), channel_id=1, source_target_pairs={{0,8},{8,16},{16,24},{24,28},{28,20},{20,12},{12,4},{4,0},{1,9},{9... | collective-permute-start | bytes 1572872 | tf_op jit(solution)/shard_map/ppermute | solution.py:68
  682.6 25.2 %collective-permute-start.60 = (bf16[128,2048]{1,0:T(8,128)(2,1)S(1)}, bf16[128,2048]{1,0:T(8,128)(2,1)}, u32[]{:S(2)}, u32[]{:S(2)}) collective-permute-start(bf16[128,2048]{1,0:T(8,128)(2,1)S(1)} %pad_maximum_fusion.14), channel_id=1, source_target_pairs={{8,0},{16,8},{24,16},{28,24},{20,28},{12,20},{4,12},{0,4},{9,1},{1... | collective-permute-start | bytes 1572872 | tf_op jit(solution)/shard_map/ppermute | solution.py:99
  689.9 14.1 %collective-permute-start.69 = (bf16[64,2048]{1,0:T(8,128)(2,1)S(1)}, bf16[64,2048]{1,0:T(8,128)(2,1)S(1)}, u32[]{:S(2)}, u32[]{:S(2)}) collective-permute-start(bf16[64,2048]{1,0:T(8,128)(2,1)S(1)} %slice.455), channel_id=1, source_target_pairs={{0,8},{8,16},{16,24},{24,28},{28,20},{20,12},{12,4},{4,0},{1,9},{9... | collective-permute-start | bytes 786440 | tf_op jit(solution)/shard_map/ppermute | solution.py:72
  703.9 14.1 %collective-permute-start.57 = (bf16[128,2048]{1,0:T(8,128)(2,1)S(1)}, bf16[128,2048]{1,0:T(8,128)(2,1)}, u32[]{:S(2)}, u32[]{:S(2)}) collective-permute-start(bf16[128,2048]{1,0:T(8,128)(2,1)S(1)} %fusion.50), channel_id=1, source_target_pairs={{0,8},{8,16},{16,24},{24,28},{28,20},{20,12},{12,4},{4,0},{1,9},{9... | collective-permute-start | bytes 1572872 | tf_op jit(solution)/shard_map/ppermute | solution.py:98
  733.6 24.7 %collective-permute-start.37 = (bf16[128,2048]{1,0:T(8,128)(2,1)}, bf16[128,2048]{1,0:T(8,128)(2,1)}, u32[]{:S(2)}, u32[]{:S(2)}) collective-permute-start(bf16[128,2048]{1,0:T(8,128)(2,1)} %get-tuple-element.113), channel_id=1, source_target_pairs={{8,0},{16,8},{24,16},{28,24},{20,28},{12,20},{4,12},{0,4},{9,1},{1... | collective-permute-start | bytes 1572872 | tf_op jit(solution)/shard_map/ppermute | solution.py:99
  746.1 16.1 %collective-permute-start.34 = (bf16[128,2048]{1,0:T(8,128)(2,1)}, bf16[128,2048]{1,0:T(8,128)(2,1)}, u32[]{:S(2)}, u32[]{:S(2)}) collective-permute-start(bf16[128,2048]{1,0:T(8,128)(2,1)} %get-tuple-element.112), channel_id=1, source_target_pairs={{0,8},{8,16},{16,24},{24,28},{28,20},{20,12},{12,4},{4,0},{1,9},{9... | collective-permute-start | bytes 1572872 | tf_op jit(solution)/shard_map/ppermute | solution.py:98
  754.6 36.8 %all-to-all-start.2 = ((bf16[8,64,768]{2,1,0:T(8,128)(2,1)}), bf16[8,64,768]{2,1,0:T(8,128)(2,1)S(1)}, u32[]{:S(2)}, u32[]{:S(2)}) async-start(bf16[8,64,768]{2,1,0:T(8,128)(2,1)} %reduce-scatter.6.cloned.1.call-done), calls=%async_computation.3 | async-start | bytes 1572864 | tf_op jit(solution)/shard_map/all_to_all | solution.py:328
  759.5 26.1 %collective-permute-start.38 = (bf16[128,2048]{1,0:T(8,128)(2,1)S(1)}, bf16[128,2048]{1,0:T(8,128)(2,1)S(1)}, u32[]{:S(2)}, u32[]{:S(2)}) collective-permute-start(bf16[128,2048]{1,0:T(8,128)(2,1)S(1)} %fusion.60), channel_id=1, source_target_pairs={{8,0},{16,8},{24,16},{28,24},{20,28},{12,20},{4,12},{0,4},{9,1},{1... | collective-permute-start | bytes 1572872 | tf_op jit(solution)/shard_map/ppermute | solution.py:99
  (132 other events, 1676.0 us)
Sparse Core Ops, SparseCore 0:
  34.6 30.8 all-gather.15
  68.4 90.9 all-gather.7
  161.0 65.7 all-gather.9
  228.2 58.2 all-gather.11
  287.9 58.2 all-gather.13
  570.7 33.8 reduce-scatter.5
  607.4 71.7 reduce-scatter.13
  681.7 73.3 reduce-scatter.11
  757.9 71.7 reduce-scatter.9
  832.7 31.4 reduce-scatter.7
